TPU v7x, 32 devices: a whole 2x2x4 slice. The times are simulated.
32 devices in a mesh: head: 4 (over x, core), blk: 8 (over z, y).
Axes of the slice: x: 2, y: 2, z: 4, core: 2. Of those that a mesh axis runs over, the one named last changes fastest.
Arguments:
- tokens: bfloat16 [16384, 768], P(('blk', 'head')), may hold values from -6 to 6
- first_values: bfloat16 [16384, 384], P(('blk', 'head')), may hold values from -6 to 6
- cotangent: bfloat16 [16384, 768], P(('blk', 'head')), may hold values from -6 to 6
- w_query: bfloat16 [768, 768], P('blk', 'head'), may hold values from -0.21875 to 0.21875
- w_key: bfloat16 [768, 768], P('blk', 'head'), may hold values from -0.21875 to 0.21875
- w_value: bfloat16 [768, 384], P('blk', 'head'), may hold values from -0.21875 to 0.21875
- w_out: bfloat16 [768, 768], P('head', 'blk'), may hold values from -3.5 to 3.5
- w_up: bfloat16 [768, 3072], P('blk', 'head'), may hold values from -0.21875 to 0.21875
- w_down: bfloat16 [3072, 768], P('head', 'blk'), may hold values from -0.109375 to 0.109375
- gain_attn: float32 [768], P('blk'), may hold values from 0.5 to 1.5
- gain_mlp: float32 [768], P('blk'), may hold values from 0.5 to 1.5
- doc_lengths: int32 [16], replicated, may hold values from 1 to 4096, 16384 in all
Outputs:
- layer_output: bfloat16 [16384, 768], P(('blk', 'head'))
- grad_tokens: float32 [16384, 768], P(('blk', 'head'))
- grad_first_values: float32 [16384, 384], P(('blk', 'head'))
- grad_w_query: float32 [768, 768], P('blk', 'head')
- grad_w_key: float32 [768, 768], P('blk', 'head')
- grad_w_value: float32 [768, 384], P('blk', 'head')
- grad_w_out: float32 [768, 768], P('head', 'blk')
- grad_w_up: float32 [768, 3072], P('blk', 'head')
- grad_w_down: float32 [3072, 768], P('head', 'blk')
- grad_gain_attn: float32 [768], P('blk')
- grad_gain_mlp: float32 [768], P('blk')
Inputs may be any that keep to these rules, and one draw needn't show every extreme that they name: `doc_lengths`: the lengths sum to 16384 and the longest is exactly 4096.
All inputs are finite; a program needn't handle non-finite values.
Results may differ from a plain program's by a relative error of at most 0.03.
Values may be sent and summed in bfloat16 or wider, within the bound.
A program may use at most 192 MiB of HBM per device.

v0:
```python
import jax
import jax.numpy as jnp
from jax import lax
from jax.sharding import PartitionSpec as P

HEADS = 12
HEAD_DIM = 64
DOC_MAX = 4096


EPSILON = 1e-05
GELU_SCALE = 0.7978845608028654
EXCLUDED = -1e30


def passed_along(block, axis, distance):
    devices = range(lax.axis_size(axis))
    route = [(i - distance, i) for i in devices if i - distance in devices]
    return lax.ppermute(block, axis, route)


def layer_norm(values, norm_gain):
    center = values - jnp.mean(values, axis=-1, keepdims=True)
    variance = jnp.mean(jnp.square(center), axis=-1, keepdims=True)
    return center * lax.rsqrt(variance + EPSILON) * norm_gain


def gelu_tanh(values):
    return (
        0.5 * values * (1.0 + jnp.tanh(GELU_SCALE * (values + 0.044715 * values * values * values)))
    )


def rows_dot(left_mat, right_mat):
    return lax.dot_general(
        left_mat, right_mat, (((0,), (0,)), ((), ())), preferred_element_type=jnp.float32
    )


def back_dot(left_mat, right_mat):
    return lax.dot_general(
        left_mat, right_mat, (((1,), (1,)), ((), ())), preferred_element_type=jnp.float32
    )


def segment_of(positions, doc_starts):
    counts = jnp.sum((doc_starts[None, :] <= positions[:, None]).astype(jnp.int32), axis=1)
    return counts - 1


def head_cols(matrix, head_index):
    return matrix[:, head_index * HEAD_DIM : (head_index + 1) * HEAD_DIM]


def on_device(
    tokens,
    first_values,
    cotangent,
    w_query,
    w_key,
    w_value,
    w_out,
    w_up,
    w_down,
    gain_attn,
    gain_mlp,
    doc_lengths,
):
    model_width = tokens.shape[1]
    half_width = model_width // 2
    head_count = lax.axis_size("head")
    local_rows = tokens.shape[0]
    block_rows = local_rows * head_count
    local_cols = model_width // head_count
    heads_here = HEADS // head_count
    score_scale = HEAD_DIM ** (-0.5)
    cycle_reach = min((DOC_MAX + block_rows - 2) // block_rows, lax.axis_size("blk") - 1)
    cycle_index = lax.axis_index("blk")
    blk_query, blk_key, blk_value, blk_out, blk_up, blk_down, attn_gain, mlp_gain = (
        lax.all_gather(w_query, "blk", axis=0, tiled=True),
        lax.all_gather(w_key, "blk", axis=0, tiled=True),
        lax.all_gather(w_value, "blk", axis=0, tiled=True),
        lax.all_gather(w_out, "blk", axis=1, tiled=True),
        lax.all_gather(w_up, "blk", axis=0, tiled=True),
        lax.all_gather(w_down, "blk", axis=1, tiled=True),
        lax.all_gather(gain_attn.astype(jnp.bfloat16), "blk", axis=0, tiled=True).astype(
            gain_attn.dtype
        ),
        lax.all_gather(gain_mlp.astype(jnp.bfloat16), "blk", axis=0, tiled=True).astype(
            gain_mlp.dtype
        ),
    )
    full_query, full_key, full_value, full_out, full_up, full_down = (
        lax.all_gather(blk_query, "head", axis=1, tiled=True),
        lax.all_gather(blk_key, "head", axis=1, tiled=True),
        lax.all_gather(blk_value, "head", axis=1, tiled=True),
        lax.all_gather(blk_out, "head", axis=0, tiled=True),
        lax.all_gather(blk_up, "head", axis=1, tiled=True),
        lax.all_gather(blk_down, "head", axis=0, tiled=True),
    )
    token_f = tokens.astype(jnp.float32)
    normed, norm_back = jax.vjp(layer_norm, token_f, attn_gain)
    normed_b = normed.astype(jnp.bfloat16)
    queries = jnp.dot(normed_b, full_query, preferred_element_type=jnp.float32).astype(jnp.bfloat16)
    keys_tok = jnp.dot(normed_b, full_key, preferred_element_type=jnp.float32).astype(jnp.bfloat16)
    fresh = jnp.dot(normed_b, full_value, preferred_element_type=jnp.float32).astype(jnp.bfloat16)
    values = jnp.concatenate([fresh, first_values], axis=1)
    query_heads, key_heads, value_heads = (
        lax.all_to_all(queries, "head", split_axis=1, concat_axis=0, tiled=True),
        lax.all_to_all(keys_tok, "head", split_axis=1, concat_axis=0, tiled=True),
        lax.all_to_all(values, "head", split_axis=1, concat_axis=0, tiled=True),
    )
    doc_ends = jnp.cumsum(doc_lengths)
    doc_starts = doc_ends - doc_lengths
    row_offsets = jnp.arange(block_rows, dtype=jnp.int32)
    query_pos = cycle_index * block_rows + row_offsets
    query_seg = segment_of(query_pos, doc_starts)
    zero_cols = jnp.zeros((block_rows, local_cols), jnp.float32)

    def tile_mask(hop_index):
        key_pos = (cycle_index - hop_index) * block_rows + row_offsets
        key_seg = segment_of(key_pos, doc_starts)
        return (key_seg[None, :] == query_seg[:, None]) & (key_pos[None, :] <= query_pos[:, None])

    def head_scores(key_block, head_index, visible_mask):
        scores = (
            jnp.einsum(
                "qd,kd->qk",
                head_cols(query_heads, head_index),
                head_cols(key_block, head_index),
                preferred_element_type=jnp.float32,
            )
            * score_scale
        )
        return jnp.where(visible_mask, scores, EXCLUDED)

    def peak_tile(row_stats, key_block, hop_index):
        row_peak, row_total = row_stats
        visible_mask = tile_mask(hop_index)
        peaks, totals = ([], [])
        for head_index in range(heads_here):
            scores = head_scores(key_block, head_index, visible_mask)
            new_peak = jnp.maximum(row_peak[head_index], jnp.max(scores, axis=1))
            totals.append(
                row_total[head_index] * jnp.exp(row_peak[head_index] - new_peak)
                + jnp.sum(jnp.exp(scores - new_peak[:, None]), axis=1)
            )
            peaks.append(new_peak)
        return (jnp.stack(peaks), jnp.stack(totals))

    own_pair = jnp.stack([key_heads, value_heads])
    first_stats = peak_tile(
        (
            jnp.full((heads_here, block_rows), EXCLUDED, jnp.float32),
            jnp.zeros((heads_here, block_rows), jnp.float32),
        ),
        key_heads,
        0,
    )

    def cycle_hop(loop_state, hop_index):
        moving, row_stats = loop_state
        moving = passed_along(moving, "blk", 1)
        row_stats = peak_tile(row_stats, moving[0], hop_index)
        return ((moving, row_stats), moving)

    (_, final_stats), kept_pairs = lax.scan(
        cycle_hop, (own_pair, first_stats), jnp.arange(1, cycle_reach + 1, dtype=jnp.int32)
    )
    log_total = final_stats[0] + jnp.log(final_stats[1])
    all_pairs = jnp.concatenate([own_pair[None], kept_pairs], axis=0)
    all_hops = jnp.arange(cycle_reach + 1, dtype=jnp.int32)

    def out_tile(key_value, hop_index):
        visible_mask = tile_mask(hop_index)
        main_parts, extra_parts = ([], [])
        for head_index in range(heads_here):
            scores = head_scores(key_value[0], head_index, visible_mask)
            soft_weights = jnp.exp(scores - log_total[head_index][:, None])
            rounded = soft_weights.astype(jnp.bfloat16)
            remainder = (soft_weights - rounded.astype(jnp.float32)).astype(jnp.bfloat16)
            value_head = head_cols(key_value[1], head_index)
            main_parts.append(jnp.dot(rounded, value_head, preferred_element_type=jnp.float32))
            extra_parts.append(jnp.dot(remainder, value_head, preferred_element_type=jnp.float32))
        return (jnp.concatenate(main_parts, axis=1), jnp.concatenate(extra_parts, axis=1))

    def out_hop(loop_state, hop_inputs):
        key_value, hop_index = hop_inputs
        main_part, extra_part = out_tile(key_value, hop_index)
        return ((loop_state[0] + main_part, loop_state[1] + extra_part), None)

    (attn_sum, attn_extra), _ = lax.scan(out_hop, (zero_cols, zero_cols), (all_pairs, all_hops))
    mixed_heads = attn_sum.astype(jnp.bfloat16)
    exact_out = attn_sum + attn_extra
    mixed = lax.all_to_all(mixed_heads, "head", split_axis=0, concat_axis=1, tiled=True)
    branch = jnp.dot(mixed, full_out, preferred_element_type=jnp.float32)
    resid = token_f + branch
    normed2, norm2_back = jax.vjp(layer_norm, resid, mlp_gain)
    normed2_b = normed2.astype(jnp.bfloat16)
    hidden_pre = jnp.dot(normed2_b, full_up, preferred_element_type=jnp.float32)
    hidden_f, gelu_back = jax.vjp(gelu_tanh, hidden_pre)
    hidden_b = hidden_f.astype(jnp.bfloat16)
    layer_output = (
        resid + jnp.dot(hidden_b, full_down, preferred_element_type=jnp.float32)
    ).astype(jnp.bfloat16)
    grad_w_down = rows_dot(hidden_b, cotangent)
    grad_hidden = back_dot(cotangent, full_down)
    grad_pre = gelu_back(grad_hidden)[0].astype(jnp.bfloat16)
    grad_w_up = rows_dot(normed2_b, grad_pre)
    grad_normed2 = back_dot(grad_pre, full_up)
    grad_resid_norm, grad_gain_m = norm2_back(grad_normed2)
    grad_resid = cotangent.astype(jnp.float32) + grad_resid_norm
    grad_branch = grad_resid.astype(jnp.bfloat16)
    grad_w_out = rows_dot(mixed, grad_branch)
    grad_mixed = back_dot(grad_branch, full_out).astype(jnp.bfloat16)
    grad_heads = lax.all_to_all(grad_mixed, "head", split_axis=1, concat_axis=0, tiled=True)
    row_delta = jnp.transpose(
        jnp.sum(
            (grad_heads.astype(jnp.float32) * exact_out).reshape(block_rows, heads_here, HEAD_DIM),
            axis=2,
        )
    )

    def grad_tile(key_value, hop_index):
        visible_mask = tile_mask(hop_index)
        query_parts, key_parts, value_parts = ([], [], [])
        for head_index in range(heads_here):
            scores = head_scores(key_value[0], head_index, visible_mask)
            soft_weights = jnp.exp(scores - log_total[head_index][:, None])
            grad_head = head_cols(grad_heads, head_index)
            grad_soft = back_dot(grad_head, head_cols(key_value[1], head_index))
            grad_scores = (soft_weights * (grad_soft - row_delta[head_index][:, None])).astype(
                jnp.bfloat16
            )
            query_parts.append(
                jnp.dot(
                    grad_scores,
                    head_cols(key_value[0], head_index),
                    preferred_element_type=jnp.float32,
                )
            )
            key_parts.append(rows_dot(grad_scores, head_cols(query_heads, head_index)))
            value_parts.append(rows_dot(soft_weights.astype(jnp.bfloat16), grad_head))
        return (
            jnp.concatenate(query_parts, axis=1),
            jnp.concatenate(key_parts, axis=1),
            jnp.concatenate(value_parts, axis=1),
        )

    def grad_part(key_value, hop_index):
        return grad_tile(key_value, hop_index)

    last_query, last_key, last_value = grad_part(all_pairs[cycle_reach], cycle_reach)

    def back_hop(loop_state, hop_inputs):
        query_grad, carried = loop_state
        key_value, hop_index = hop_inputs
        carried = passed_along(carried.astype(jnp.bfloat16), "blk", -1).astype(carried.dtype)
        part_query, part_key, part_value = grad_part(key_value, hop_index)
        return ((query_grad + part_query, carried + jnp.stack([part_key, part_value])), None)

    (query_grad, carried), _ = lax.scan(
        back_hop,
        (last_query, jnp.stack([last_key, last_value])),
        (
            jnp.flip(all_pairs[:cycle_reach], axis=0),
            jnp.arange(cycle_reach - 1, -1, -1, dtype=jnp.int32),
        ),
    )
    grad_q_heads = (query_grad * score_scale).astype(jnp.bfloat16)
    grad_k_heads = (carried[0] * score_scale).astype(jnp.bfloat16)
    grad_v_heads = carried[1].astype(jnp.bfloat16)
    grad_query, grad_key, grad_values = (
        lax.all_to_all(grad_q_heads, "head", split_axis=0, concat_axis=1, tiled=True),
        lax.all_to_all(grad_k_heads, "head", split_axis=0, concat_axis=1, tiled=True),
        lax.all_to_all(grad_v_heads, "head", split_axis=0, concat_axis=1, tiled=True),
    )
    grad_fresh = grad_values[:, :half_width]
    grad_first = grad_values[:, half_width:].astype(jnp.float32)
    whole_query = rows_dot(normed_b, grad_query)
    whole_key = rows_dot(normed_b, grad_key)
    whole_value = rows_dot(normed_b, grad_fresh)
    grad_normed = (
        back_dot(grad_query, full_query)
        + back_dot(grad_key, full_key)
        + back_dot(grad_fresh, full_value)
    )
    grad_token_norm, grad_gain_a = norm_back(grad_normed)
    grad_tokens = grad_resid + grad_token_norm
    (
        grad_w_query,
        grad_w_key,
        grad_w_value,
        grad_w_out,
        grad_w_up,
        grad_w_down,
        gain_a_term,
        gain_m_term,
    ) = (
        lax.psum_scatter(
            whole_query.astype(jnp.bfloat16), "head", scatter_dimension=1, tiled=True
        ).astype(jnp.float32),
        lax.psum_scatter(
            whole_key.astype(jnp.bfloat16), "head", scatter_dimension=1, tiled=True
        ).astype(jnp.float32),
        lax.psum_scatter(
            whole_value.astype(jnp.bfloat16), "head", scatter_dimension=1, tiled=True
        ).astype(jnp.float32),
        lax.psum_scatter(
            grad_w_out.astype(jnp.bfloat16), "head", scatter_dimension=0, tiled=True
        ).astype(jnp.float32),
        lax.psum_scatter(
            grad_w_up.astype(jnp.bfloat16), "head", scatter_dimension=1, tiled=True
        ).astype(jnp.float32),
        lax.psum_scatter(
            grad_w_down.astype(jnp.bfloat16), "head", scatter_dimension=0, tiled=True
        ).astype(jnp.float32),
        lax.psum_scatter(
            jnp.tile(grad_gain_a, head_count).astype(jnp.bfloat16),
            "head",
            scatter_dimension=0,
            tiled=True,
        ).astype(jnp.float32),
        lax.psum_scatter(
            jnp.tile(grad_gain_m, head_count).astype(jnp.bfloat16),
            "head",
            scatter_dimension=0,
            tiled=True,
        ).astype(jnp.float32),
    )
    (
        final_query,
        final_key,
        final_value,
        final_out,
        final_up,
        final_down,
        out_gain_attn,
        out_gain_mlp,
    ) = (
        lax.psum_scatter(
            grad_w_query.astype(jnp.bfloat16), "blk", scatter_dimension=0, tiled=True
        ).astype(jnp.float32),
        lax.psum_scatter(
            grad_w_key.astype(jnp.bfloat16), "blk", scatter_dimension=0, tiled=True
        ).astype(jnp.float32),
        lax.psum_scatter(
            grad_w_value.astype(jnp.bfloat16), "blk", scatter_dimension=0, tiled=True
        ).astype(jnp.float32),
        lax.psum_scatter(
            grad_w_out.astype(jnp.bfloat16), "blk", scatter_dimension=1, tiled=True
        ).astype(jnp.float32),
        lax.psum_scatter(
            grad_w_up.astype(jnp.bfloat16), "blk", scatter_dimension=0, tiled=True
        ).astype(jnp.float32),
        lax.psum_scatter(
            grad_w_down.astype(jnp.bfloat16), "blk", scatter_dimension=1, tiled=True
        ).astype(jnp.float32),
        lax.psum_scatter(
            gain_a_term.astype(jnp.bfloat16), "blk", scatter_dimension=0, tiled=True
        ).astype(jnp.float32),
        lax.psum_scatter(
            gain_m_term.astype(jnp.bfloat16), "blk", scatter_dimension=0, tiled=True
        ).astype(jnp.float32),
    )
    return (
        layer_output,
        grad_tokens,
        grad_first,
        final_query,
        final_key,
        final_value,
        final_out,
        final_up,
        final_down,
        out_gain_attn,
        out_gain_mlp,
    )


def solution(mesh):
    in_specs = (
        P(("blk", "head"), None),
        P(("blk", "head"), None),
        P(("blk", "head"), None),
        P("blk", "head"),
        P("blk", "head"),
        P("blk", "head"),
        P("head", "blk"),
        P("blk", "head"),
        P("head", "blk"),
        P("blk"),
        P("blk"),
        P(),
    )
    out_specs = (
        P(("blk", "head"), None),
        P(("blk", "head"), None),
        P(("blk", "head"), None),
        P("blk", "head"),
        P("blk", "head"),
        P("blk", "head"),
        P("head", "blk"),
        P("blk", "head"),
        P("head", "blk"),
        P("blk"),
        P("blk"),
    )
    return jax.shard_map(
        on_device, mesh=mesh, in_specs=in_specs, out_specs=out_specs, check_vma=False
    )
```

profile of v0, /device:TPU:0, one launch (start us, length us, event | category | flops | bytes accessed | tf_op | source)
XLA Modules:
  0.0 1675.3 jit_solution(4247412954536712824)
XLA Ops:
  8.0 33.2 %all_gather.43 = bf16[768,192]{1,0:T(8,128)(2,1)S(1)} all-gather(bf16[96,192]{1,0:T(8,128)(2,1)} %param.22), channel_id=1, replica_groups=mesh['head'=4,'blk'=8] {'blk'}, dimensions={0}, use_global_device_ids=true | all-gather | bytes 331776 | tf_op jit(solution)/shard_map/all_gather | solution.py:81
  42.1 31.5 %all_gather.47 = bf16[768,192]{1,0:T(8,128)(2,1)S(1)} all-gather(bf16[96,192]{1,0:T(8,128)(2,1)} %param.21), channel_id=1, replica_groups=mesh['head'=4,'blk'=8] {'blk'}, dimensions={0}, use_global_device_ids=true | all-gather | bytes 331776 | tf_op jit(solution)/shard_map/all_gather | solution.py:80
  76.0 31.0 %all_gather.49 = bf16[192,768]{0,1:T(8,128)(2,1)S(1)} all-gather(bf16[192,96]{0,1:T(8,128)(2,1)S(1)} %copy.178), channel_id=1, replica_groups=mesh['head'=4,'blk'=8] {'blk'}, dimensions={1}, use_global_device_ids=true | all-gather | bytes 331776 | tf_op jit(solution)/shard_map/all_gather | solution.py:83
  112.3 21.9 %all-reduce.7 = (bf16[768]{0:T(1024)(128)(2,1)S(1)}, bf16[768]{0:T(1024)(128)(2,1)S(1)}) all-reduce(bf16[768]{0:T(1024)(128)(2,1)S(1)} %dynamic-update-slice, bf16[768]{0:T(1024)(128)(2,1)S(1)} %dynamic-update-slice.1), channel_id=1, replica_groups=mesh['head'=4,'blk'=8] {'blk'}, use_global_device_ids=true, to_apply=%add | all-reduce | flops 1536 | bytes 6144
  134.2 30.8 %all_gather.45 = bf16[768,96]{1,0:T(8,128)(2,1)S(1)} all-gather(bf16[96,96]{1,0:T(8,128)(2,1)} %param.23), channel_id=1, replica_groups=mesh['head'=4,'blk'=8] {'blk'}, dimensions={0}, use_global_device_ids=true | all-gather | bytes 165888 | tf_op jit(solution)/shard_map/all_gather | solution.py:82
  165.9 11.1 all_gather.46
  186.3 17.0 %all-to-all-done.1 = bf16[512,4,192]{0,2,1:T(8,128)(2,1)S(1)} async-done(((bf16[512,4,192]{0,2,1:T(8,128)(2,1)}), bf16[512,4,192]{0,2,1:T(8,128)(2,1)S(1)}, u32[]{:S(2)}, u32[]{:S(2)}) %all-to-all-start.1) | async-done | bytes 786464 | tf_op jit(solution)/shard_map/all_to_all | solution.py:111
  254.5 18.6 %exponential_reduce_fusion.5 = (f32[2048]{0:T(1024)S(1)}, f32[2048]{0:T(1024)S(1)}, f32[2048]{0:T(1024)S(1)}, f32[2048,2048]{0,1:T(8,128)}) fusion(f32[2048,2048]{0,1:T(8,128)} %get-tuple-element.963, f32[2048]{0:T(1024)S(1)} %broadcast_maximum_fusion.2, s32[2048]{0:T(1024)S(1)} %iota_add_fusion.7, s32[2048]{0:T(1024)S(1)} %get-tuple-element.1345, ...), kind=kOutput, calls=%fused_computation.181 | convolution fusion | flops 591390720 | bytes 50921472 | tf_op jit(solution)/shard_map/qd,kd->qk/dot_general | solution.py:127
  273.2 13.9 exponential_reduce_fusion.4
  287.3 178.9 %while.49 = (s32[]{:T(128)}, bf16[2,2048,192]{1,2,0:T(8,128)(2,1)}, f32[3,2048]{1,0:T(4,128)S(1)}, f32[3,2048]{1,0:T(4,128)S(1)}, bf16[2,2,2048,192]{2,3,1,0:T(8...) while((s32[]{:T(128)}, bf16[2,2048,192]{1,2,0:T(8,128)(2,1)}, ...), condition=%wide.region_18.19_spmd.clone, body=%wide.region_10.18_spmd.clone.sunk | while | flops 1736587264 | bytes 159712272 | solution.py:167
  290.3 32.5 %collective-permute-done = bf16[2,2048,192]{1,2,0:T(8,128)(2,1)S(1)} collective-permute-done((bf16[2,2048,192]{1,2,0:T(8,128)(2,1)}, bf16[2,2048,192]{1,2,0:T(8,128)(2,1)S(1)}, u32[]{:S(2)}, u32[]{:S(2)}) %collective-permute-start) | collective-permute-done | bytes 1572896 | tf_op jit(solution)/shard_map/while/body/eval_jaxpr/ppermute | solution.py:19
  339.1 19.3 %exponential_reduce_fusion.8 = (f32[2048]{0:T(1024)S(1)}, f32[2048]{0:T(1024)S(1)}, f32[2048]{0:T(1024)S(1)}, f32[2048,2048]{0,1:T(8,128)}) fusion(f32[2048,2048]{0,1:T(8,128)} %get-tuple-element.1199, f32[2048]{0:T(1024)} %max.69, s32[2048]{0:T(1024)S(1)} %get-tuple-element.1197, s32[2048]{0:T(1024)S(1)} %get-tuple-element.1198, ...), kind=kOutput, calls=%fused_computation.8.clone.1 | convolution fusion | flops 591390720 | bytes 51183616 | tf_op jit(solution)/shard_map/while/body/eval_jaxpr/qd,kd->qk/dot_general | solution.py:127
  358.5 14.0 exponential_reduce_fusion.9
  381.6 31.7 %collective-permute-done = bf16[2,2048,192]{1,2,0:T(8,128)(2,1)S(1)} collective-permute-done((bf16[2,2048,192]{1,2,0:T(8,128)(2,1)}, bf16[2,2048,192]{1,2,0:T(8,128)(2,1)S(1)}, u32[]{:S(2)}, u32[]{:S(2)}) %collective-permute-start) | collective-permute-done | bytes 1572896 | tf_op jit(solution)/shard_map/while/body/eval_jaxpr/ppermute | solution.py:19
  429.5 19.3 %exponential_reduce_fusion.8 = (f32[2048]{0:T(1024)S(1)}, f32[2048]{0:T(1024)S(1)}, f32[2048]{0:T(1024)S(1)}, f32[2048,2048]{0,1:T(8,128)}) fusion(f32[2048,2048]{0,1:T(8,128)} %get-tuple-element.1199, f32[2048]{0:T(1024)} %max.69, s32[2048]{0:T(1024)S(1)} %get-tuple-element.1197, s32[2048]{0:T(1024)S(1)} %get-tuple-element.1198, ...), kind=kOutput, calls=%fused_computation.8.clone.1 | convolution fusion | flops 591390720 | bytes 51183616 | tf_op jit(solution)/shard_map/while/body/eval_jaxpr/qd,kd->qk/dot_general | solution.py:127
  448.9 14.0 exponential_reduce_fusion.9
  478.9 157.4 %while.51 = (s32[]{:T(128)}, f32[2048,192]{0,1:T(8,128)S(1)}, f32[2048,192]{0,1:T(8,128)}, s32[16]{0:T(128)S(1)}, s32[3]{0:T(128)S(1)}, /*index=5*/s32[]{:T(128)...) while((s32[]{:T(128)}, f32[2048,192]{0,1:T(8,128)S(1)}, ...), condition=%wide.region_21.22_spmd.clone, body=%wide.region_19.21_spmd.clone.sunk | while | flops 5048995840 | bytes 185942384 | solution.py:192
  680.9 13.2 fusion.147
  738.6 9.8 multiply_convert_fusion
  761.7 10.0 multiply_convert_fusion.1
  785.0 9.8 multiply_convert_fusion.2
  802.5 241.9 %while.50 = (s32[]{:T(128)}, f32[2048,192]{0,1:T(8,128)}, f32[2,2048,192]{1,2,0:T(8,128)}, s32[16]{0:T(128)S(1)}, s32[2]{0:T(128)S(1)}, /*index=5*/s32[]{:T(128)...) while((s32[]{:T(128)}, f32[2048,192]{0,1:T(8,128)}, ...), condition=%wide.region_30.31_spmd.clone, body=%wide.region_28.30_spmd.clone.sunk | while | flops 8260390912 | bytes 378692768 | solution.py:262
  843.8 9.6 fusion.387
  874.9 9.8 fusion.390
  884.7 9.9 fusion.384
  898.2 9.7 fusion.389
  907.9 12.1 fusion.381
  948.7 9.6 fusion.387
  979.7 9.8 fusion.390
  989.5 9.9 fusion.384
  1003.1 9.7 fusion.389
  1012.8 12.1 fusion.381
  1046.8 14.1 all_to_all.143
  1068.1 14.1 all_to_all.144
  1089.9 14.1 all_to_all.145
  1126.7 20.5 %reduce-scatter.23.cloned.1.call-done = bf16[768,192]{0,1:T(8,128)(2,1)} async-done(((bf16[768,768]{0,1:T(8,128)(2,1)}), bf16[768,192]{0,1:T(8,128)(2,1)}) %reduce-scatter.23.cloned.1.call-update) | async-done | bytes 294928 | tf_op jit(solution)/shard_map/reduce_scatter | solution.py:300
  1149.2 26.4 %reduce-scatter.25.cloned.1.call-done = bf16[768,192]{0,1:T(8,128)(2,1)} async-done(((bf16[768,768]{0,1:T(8,128)(2,1)}), bf16[768,192]{0,1:T(8,128)(2,1)}) %reduce-scatter.25.cloned.1.call-update) | async-done | bytes 294928 | tf_op jit(solution)/shard_map/reduce_scatter | solution.py:303
  1177.6 48.5 %reduce-scatter.35.cloned.1.call-done = bf16[768,768]{1,0:T(8,128)(2,1)} async-done(((bf16[3072,768]{1,0:T(8,128)(2,1)}), bf16[768,768]{1,0:T(8,128)(2,1)}) %reduce-scatter.35.cloned.1.call-update) | async-done | bytes 1179664 | tf_op jit(solution)/shard_map/reduce_scatter | solution.py:315
  1230.6 9.7 add_convert_fusion
  1240.3 36.1 %reduce-scatter.31.cloned.1.call-done = bf16[768,768]{1,0:T(8,128)(2,1)} async-done(((bf16[768,3072]{1,0:T(8,128)(2,1)}), bf16[768,768]{1,0:T(8,128)(2,1)}) %reduce-scatter.31.cloned.1.call-update) | async-done | bytes 1179664 | tf_op jit(solution)/shard_map/reduce_scatter | solution.py:312
  1284.8 10.1 all-reduce.8
  1299.4 21.4 %all-reduce.6 = (bf16[768]{0:T(1024)(128)(2,1)S(1)}, bf16[768]{0:T(1024)(128)(2,1)S(1)}) all-reduce(bf16[768]{0:T(1024)(128)(2,1)S(1)} %dynamic-slice.3, bf16[768]{0:T(1024)(128)(2,1)S(1)} %dynamic-slice.7), channel_id=15, replica_groups=mesh['head'=4,'blk'=8] {'blk'}, use_global_device_ids=true, to_apply=%region_47.48.clone | all-reduce | flops 1536 | bytes 6144
  1325.2 16.4 reduce-scatter.41.cloned.1.call-done
  1343.2 62.3 %reduce-scatter.43.cloned.1.call-done = bf16[96,192]{1,0:T(8,128)(2,1)} async-done(((bf16[768,192]{1,0:T(8,128)(2,1)}), bf16[96,192]{1,0:T(8,128)(2,1)}) %reduce-scatter.43.cloned.1.call-update) | async-done | bytes 36880
  1407.0 62.3 %reduce-scatter.37.cloned.1.call-done = bf16[96,192]{1,0:T(8,128)(2,1)} async-done(((bf16[768,192]{1,0:T(8,128)(2,1)}), bf16[96,192]{1,0:T(8,128)(2,1)}) %reduce-scatter.37.cloned.1.call-update) | async-done | bytes 36880
  1471.0 62.2 %reduce-scatter.39.cloned.1.call-done = bf16[96,192]{1,0:T(8,128)(2,1)} async-done(((bf16[768,192]{1,0:T(8,128)(2,1)}), bf16[96,192]{1,0:T(8,128)(2,1)}) %reduce-scatter.39.cloned.1.call-update) | async-done | bytes 36880
  1534.9 65.1 %reduce-scatter.45.cloned.1.call-done = bf16[96,768]{1,0:T(8,128)(2,1)} async-done(((bf16[768,768]{1,0:T(8,128)(2,1)}), bf16[96,768]{1,0:T(8,128)(2,1)}) %reduce-scatter.45.cloned.1.call-update) | async-done | bytes 147472
  1601.9 64.9 %reduce-scatter.33.cloned.1.call-done = bf16[96,768]{1,0:T(8,128)(2,1)} async-done(((bf16[768,768]{1,0:T(8,128)(2,1)}), bf16[96,768]{1,0:T(8,128)(2,1)}) %reduce-scatter.33.cloned.1.call-update) | async-done | bytes 147472 | tf_op jit(solution)/shard_map/reduce_scatter | solution.py:353
  (572 shorter events, 568.2 us)
Async XLA Ops:
  7.2 158.0 %copy-start.50 = (bf16[512,384]{1,0:T(8,128)(2,1)S(1)}, bf16[512,384]{1,0:T(8,128)(2,1)}, u32[]{:S(2)}) copy-start(bf16[512,384]{1,0:T(8,128)(2,1)} %param.19) | copy-start | bytes 1179652
  7.2 158.2 %copy-start.13 = (bf16[512,768]{1,0:T(8,128)(2,1)S(1)}, bf16[512,768]{1,0:T(8,128)(2,1)}, u32[]{:S(2)}) copy-start(bf16[512,768]{1,0:T(8,128)(2,1)} %param.18) | copy-start | bytes 2359300
  7.2 100.8 %all-gather.18.cloned.1.call-start = ((), (), s32[]{:S(2)}) async-start(), calls=%async_computation.25 | async-start | bytes 1327104 | tf_op jit(solution)/shard_map/all_gather | solution.py:85
  7.9 175.0 %all-gather.8.cloned.1.call-start = ((), (), s32[]{:S(2)}) async-start(), calls=%async_computation.20 | async-start | bytes 1474560 | tf_op jit(solution)/shard_map/all_gather | solution.py:95
  42.1 164.8 %all-gather.10.cloned.1.call-start = ((), (), s32[]{:S(2)}) async-start(), calls=%async_computation.21 | async-start | bytes 1474560 | tf_op jit(solution)/shard_map/all_gather | solution.py:94
  74.5 151.1 %all-gather.14.cloned.1.call-start = ((), (), s32[]{:S(2)}) async-start(), calls=%async_computation.23 | async-start | bytes 1327104 | tf_op jit(solution)/shard_map/all_gather | solution.py:84
  75.1 594.0 %all-gather.12.cloned.1.call-start = ((), (), s32[]{:S(2)}) async-start(), calls=%async_computation.22 | async-start | bytes 1474560 | tf_op jit(solution)/shard_map/all_gather | solution.py:97
  107.9 565.1 %all-gather.20.cloned.1.call-start = ((), (), s32[]{:S(2)}) async-start(), calls=%async_computation.26 | async-start | bytes 5898240 | tf_op jit(solution)/shard_map/all_gather | solution.py:99
  134.2 72.7 %copy-start.60 = (f32[768]{0:T(1024)}, f32[768]{0:T(1024)S(1)}, u32[]{:S(2)}) copy-start(f32[768]{0:T(1024)S(1)} %convert_element_type.292) | copy-start | bytes 9220
  165.5 41.4 %copy-start.62 = (f32[512]{0:T(512)}, f32[512]{0:T(512)S(1)}, u32[]{:S(2)}) copy-start(f32[512]{0:T(512)S(1)} %broadcast_multiply_fusion.1) | copy-start | bytes 6148
  177.8 29.1 %copy-start.66 = (f32[512]{0:T(512)}, f32[512]{0:T(512)S(1)}, u32[]{:S(2)}) copy-start(f32[512]{0:T(512)S(1)} %fusion.204) | copy-start | bytes 6148
  179.4 23.9 %all-to-all-start.1 = ((bf16[512,4,192]{0,2,1:T(8,128)(2,1)}), bf16[512,4,192]{0,2,1:T(8,128)(2,1)S(1)}, u32[]{:S(2)}, u32[]{:S(2)}) async-start(bf16[512,4,192]{0,2,1:T(8,128)(2,1)} %bitcast.4), calls=%async_computation.1 | async-start | bytes 1572864 | tf_op jit(solution)/shard_map/all_to_all | solution.py:111
  185.1 38.3 %copy-start.80 = (s32[16]{0:T(128)S(1)}, s32[16]{0:T(128)}, u32[]{:S(2)}) copy-start(s32[16]{0:T(128)} %param.29) | copy-start | bytes 196
  203.3 15.1 all-to-all-start
  206.9 66.3 %copy-start.53 = (s32[2048]{0:T(1024)}, s32[2048]{0:T(1024)S(1)}, u32[]{:S(2)}) copy-start(s32[2048]{0:T(1024)S(1)} %iota_add_fusion.7) | copy-start | bytes 24580
  218.4 15.1 all-to-all-start.2
  221.9 458.9 %all-gather.16.cloned.1.call-start = ((), (), s32[]{:S(2)}) async-start(), calls=%async_computation.24 | async-start | bytes 5898240 | tf_op jit(solution)/shard_map/all_gather | solution.py:98
  287.5 35.3 %collective-permute-start = (bf16[2,2048,192]{1,2,0:T(8,128)(2,1)}, bf16[2,2048,192]{1,2,0:T(8,128)(2,1)S(1)}, u32[]{:S(2)}, u32[]{:S(2)}) collective-permute-start(bf16[2,2048,192]{1,2,0:T(8,128)(2,1)} %get-tuple-element.1269), channel_id=1, source_target_pairs={{0,1},{1,2},{2,3},{3,4},{4,5},{5,6},{6,7},{8,9},{9,10},{10,11},{11... | collective-permute-start | bytes 4718600 | tf_op jit(solution)/shard_map/while/body/eval_jaxpr/ppermute | solution.py:19
  375.8 37.5 %collective-permute-start = (bf16[2,2048,192]{1,2,0:T(8,128)(2,1)}, bf16[2,2048,192]{1,2,0:T(8,128)(2,1)S(1)}, u32[]{:S(2)}, u32[]{:S(2)}) collective-permute-start(bf16[2,2048,192]{1,2,0:T(8,128)(2,1)} %get-tuple-element.1269), channel_id=1, source_target_pairs={{0,1},{1,2},{2,3},{3,4},{4,5},{5,6},{6,7},{8,9},{9,10},{10,11},{11... | collective-permute-start | bytes 4718600 | tf_op jit(solution)/shard_map/while/body/eval_jaxpr/ppermute | solution.py:19
  646.1 23.0 %all-to-all-start.3 = ((bf16[4,512,192]{1,2,0:T(8,128)(2,1)}), bf16[4,512,192]{1,2,0:T(8,128)(2,1)}, u32[]{:S(2)}, u32[]{:S(2)}) async-start(bf16[4,512,192]{1,2,0:T(8,128)(2,1)} %bitcast.235), calls=%async_computation.3 | async-start | bytes 1572864 | tf_op jit(solution)/shard_map/all_to_all | solution.py:195
  671.5 26.0 %copy-start.70 = (f32[512]{0:T(512)}, f32[512]{0:T(512)S(1)}, u32[]{:S(2)}) copy-start(f32[512]{0:T(512)S(1)} %broadcast_multiply_fusion) | copy-start | bytes 6148
  673.0 24.5 %copy-start.76 = (f32[512]{0:T(512)}, f32[512]{0:T(512)S(1)}, u32[]{:S(2)}) copy-start(f32[512]{0:T(512)S(1)} %fusion.205) | copy-start | bytes 6148
  704.4 15.9 all-to-all-start.4
  708.6 414.3 %reduce-scatter.27.cloned.1.call-start = ((), (), s32[]{:S(2)}) async-start(), calls=%async_computation.29 | async-start | bytes 737280 | tf_op jit(solution)/shard_map/reduce_scatter | solution.py:306
  829.4 97.4 %collective-permute-start.1 = (bf16[2,2048,192]{1,2,0:T(8,128)(2,1)}, bf16[2,2048,192]{1,2,0:T(8,128)(2,1)}, u32[]{:S(2)}, u32[]{:S(2)}) collective-permute-start(bf16[2,2048,192]{1,2,0:T(8,128)(2,1)} %convert_element_type.515), channel_id=1, source_target_pairs={{1,0},{2,1},{3,2},{4,3},{5,4},{6,5},{7,6},{9,8},{10,9},{11,10},{12... | collective-permute-start | bytes 4718600 | tf_op jit(solution)/shard_map/while/body/eval_jaxpr/ppermute | solution.py:19
  832.0 66.2 %copy-start.51 = (s32[2048]{0:T(1024)}, s32[2048]{0:T(1024)S(1)}, u32[]{:S(2)}) copy-start(s32[2048]{0:T(1024)S(1)} %iota_add_fusion.15) | copy-start | bytes 24580 | tf_op jit(solution)/shard_map/while
  832.1 66.1 %copy-start.52 = (s32[2048]{0:T(1024)}, s32[2048]{0:T(1024)S(1)}, u32[]{:S(2)}) copy-start(s32[2048]{0:T(1024)S(1)} %broadcast_add_fusion.9) | copy-start | bytes 24580 | tf_op jit(solution)/shard_map/while
  934.3 97.4 %collective-permute-start.1 = (bf16[2,2048,192]{1,2,0:T(8,128)(2,1)}, bf16[2,2048,192]{1,2,0:T(8,128)(2,1)}, u32[]{:S(2)}, u32[]{:S(2)}) collective-permute-start(bf16[2,2048,192]{1,2,0:T(8,128)(2,1)} %convert_element_type.515), channel_id=1, source_target_pairs={{1,0},{2,1},{3,2},{4,3},{5,4},{6,5},{7,6},{9,8},{10,9},{11,10},{12... | collective-permute-start | bytes 4718600 | tf_op jit(solution)/shard_map/while/body/eval_jaxpr/ppermute | solution.py:19
  936.8 66.2 %copy-start.51 = (s32[2048]{0:T(1024)}, s32[2048]{0:T(1024)S(1)}, u32[]{:S(2)}) copy-start(s32[2048]{0:T(1024)S(1)} %iota_add_fusion.15) | copy-start | bytes 24580 | tf_op jit(solution)/shard_map/while
  937.0 66.1 %copy-start.52 = (s32[2048]{0:T(1024)}, s32[2048]{0:T(1024)S(1)}, u32[]{:S(2)}) copy-start(s32[2048]{0:T(1024)S(1)} %broadcast_add_fusion.9) | copy-start | bytes 24580 | tf_op jit(solution)/shard_map/while
  1063.3 61.4 %reduce-scatter.29.cloned.1.call-start = ((), (), s32[]{:S(2)}) async-start(), calls=%async_computation.30 | async-start | bytes 1474560 | tf_op jit(solution)/shard_map/reduce_scatter | solution.py:309
  1066.3 80.9 %reduce-scatter.23.cloned.1.call-start = ((), (), s32[]{:S(2)}) async-start(), calls=%async_computation.27 | async-start | bytes 1474560 | tf_op jit(solution)/shard_map/reduce_scatter | solution.py:300
  1086.3 89.2 %reduce-scatter.25.cloned.1.call-start = ((), (), s32[]{:S(2)}) async-start(), calls=%async_computation.28 | async-start | bytes 1474560 | tf_op jit(solution)/shard_map/reduce_scatter | solution.py:303
  1107.5 118.5 %reduce-scatter.35.cloned.1.call-start = ((), (), s32[]{:S(2)}) async-start(), calls=%async_computation.33 | async-start | bytes 5898240 | tf_op jit(solution)/shard_map/reduce_scatter | solution.py:315
  1116.2 160.2 %reduce-scatter.31.cloned.1.call-start = ((), (), s32[]{:S(2)}) async-start(), calls=%async_computation.31 | async-start | bytes 5898240 | tf_op jit(solution)/shard_map/reduce_scatter | solution.py:312
  1122.8 105.9 %copy-start.83 = (u32[32]{0:T(128)S(1)}, u32[32]{0:T(128)}, u32[]{:S(2)}) copy-start(u32[32]{0:T(128)} %constant.193) | copy-start | bytes 388
  1122.8 107.8 %copy-start.79 = (bf16[768]{0:T(1024)(128)(2,1)S(1)}, bf16[768]{0:T(1024)(128)(2,1)}, u32[]{:S(2)}) copy-start(bf16[768]{0:T(1024)(128)(2,1)} %get-tuple-element.827) | copy-start | bytes 4612
  1122.8 218.8 %reduce-scatter.41.cloned.1.call-start = ((), (), s32[]{:S(2)}) async-start(), calls=%async_computation.36 | async-start | bytes 221184
  1124.7 280.8 %reduce-scatter.43.cloned.1.call-start = ((), (), s32[]{:S(2)}) async-start(), calls=%async_computation.37 | async-start | bytes 442368
  1126.7 342.7 %reduce-scatter.37.cloned.1.call-start = ((), (), s32[]{:S(2)}) async-start(), calls=%async_computation.34 | async-start | bytes 442368
  1149.2 384.1 %reduce-scatter.39.cloned.1.call-start = ((), (), s32[]{:S(2)}) async-start(), calls=%async_computation.35 | async-start | bytes 442368
  1177.5 422.5 %reduce-scatter.45.cloned.1.call-start = ((), (), s32[]{:S(2)}) async-start(), calls=%async_computation.38 | async-start | bytes 1327104
  1228.4 438.4 %reduce-scatter.33.cloned.1.call-start = ((), (), s32[]{:S(2)}) async-start(), calls=%async_computation.32 | async-start | bytes 1327104 | tf_op jit(solution)/shard_map/reduce_scatter | solution.py:353
  1230.6 45.8 %copy-start.44 = (bf16[4,512,192]{1,2,0:T(8,128)(2,1)S(1)}, bf16[4,512,192]{1,2,0:T(8,128)(2,1)}, u32[]{:S(2)}) copy-start(bf16[4,512,192]{1,2,0:T(8,128)(2,1)} %copy-done.43) | copy-start | bytes 2359300
  1240.3 38.2 %copy-start.46 = (bf16[4,512,192]{1,2,0:T(8,128)(2,1)S(1)}, bf16[4,512,192]{1,2,0:T(8,128)(2,1)}, u32[]{:S(2)}) copy-start(bf16[4,512,192]{1,2,0:T(8,128)(2,1)} %copy-done.45) | copy-start | bytes 2359300
  1240.3 40.3 %copy-start.16 = (bf16[512,768]{1,0:T(8,128)(2,1)S(1)}, bf16[512,768]{1,0:T(8,128)(2,1)}, u32[]{:S(2)}) copy-start(bf16[512,768]{1,0:T(8,128)(2,1)} %param.18) | copy-start | bytes 2359300
  1280.7 41.3 %copy-start.20 = (f32[512,768]{1,0:T(8,128)S(1)}, f32[512,768]{1,0:T(8,128)}, u32[]{:S(2)}) copy-start(f32[512,768]{1,0:T(8,128)} %copy-done.19) | copy-start | bytes 4718596
  1280.7 41.3 %copy-start.69 = (f32[512]{0:T(512)S(1)}, f32[512]{0:T(512)}, u32[]{:S(2)}) copy-start(f32[512]{0:T(512)} %copy-done.68) | copy-start | bytes 6148
  (97 other events, 701.5 us)
Sparse Core Ops, SparseCore 0:
  10.2 46.6 all-gather.17
  59.1 15.6 all-gather.7
  76.9 17.4 all-gather.9
  96.4 41.6 all-gather.13
  139.5 16.2 all-gather.11
  157.2 49.0 all-gather.19
  225.7 35.1 all-gather.15
  1063.4 26.3 reduce-scatter.26
  1092.4 26.4 reduce-scatter.28
  1121.5 25.6 reduce-scatter.22
  1149.8 25.7 reduce-scatter.24
  1178.1 47.8 reduce-scatter.34
  1228.5 47.8 reduce-scatter.30
  1280.5 61.1 reduce-scatter.40
  1345.1 60.3 reduce-scatter.42
  1408.9 60.3 reduce-scatter.36
  1472.8 60.3 reduce-scatter.38
  1536.9 63.0 reduce-scatter.44
  1603.8 63.0 reduce-scatter.32
where the time goes:
time: 1680 us
  matrix products  578 us (34%)
  waiting for transfers between devices  562 us (33%)
  blocking collectives  233 us (14%)
  other arithmetic  101 us (6%)
  local copies, waits for them, and re-layouts  98.7 us (6%)
  loops' own time  56.1 us (3%)
  starting transfers between devices  28.4 us (2%)
  between operations  17.4 us (1%)
    unnamed x24, waiting for transfers between devices  270 us
    dot_general x27, matrix products, head_scores(): jnp.einsum('qd,kd->qk', head_cols(query_heads, head_index), head_cols(key...  187 us
    dot_general x24, matrix products, rows_dot(): lax.dot_general(left_mat, right_mat, (((0,), (0,)), ((), ())), preferred_...  130 us
    dot_general x15, matrix products, back_dot(): lax.dot_general(left_mat, right_mat, (((1,), (1,)), ((), ())), preferred_...  112 us
    reduce_scatter x1, waiting for transfers between devices, on_device(): lax.psum_scatter(grad_w_up.astype(jnp.bfloat16), 'blk', scatter_dimension...  64.9 us
    ppermute x4, waiting for transfers between devices, passed_along(): return lax.ppermute(block, axis, route)  64.2 us
    unnamed x3, blocking collectives  53.4 us
    dot_general x9, matrix products, out_tile(): jnp.dot(remainder, value_head, preferred_element_type=jnp.float32)  52.2 us
  transfers between devices with their start and end apart: 28, of which 16 were waited for; matrix products, arithmetic and copies ran while one was open for 38% of the time, Pallas kernels for 0%

commit v1 on v0

v1 whole, which is shorter than its diff:
```python
import functools

import jax
import jax.numpy as jnp
from jax import lax
from jax.experimental import pallas as pl
from jax.experimental.pallas import tpu as pltpu
from jax.sharding import PartitionSpec as P

HEADS = 12
HEAD_DIM = 64
DOC_MAX = 4096
EPSILON = 1e-05
GELU_SCALE = 0.7978845608028654
EXCLUDED = -1e30
WIDTH = 256
SPLITS = 3
BF16 = jnp.bfloat16
F32 = jnp.float32
MESH = pl.DeviceIdType.MESH
ANY = pl.BlockSpec(memory_space=pl.ANY)
WHOLE = pl.BlockSpec(memory_space=pltpu.VMEM)
NT = (((1,), (1,)), ((), ()))
TN = (((0,), (0,)), ((), ()))


def dotf(left, right, dims=None):
    if dims is None:
        dims = (((1,), (0,)), ((), ()))
    return lax.dot_general(left, right, dims, preferred_element_type=F32)


def remote(src, dst, send_sem, recv_sem, head, blk):
    return pltpu.make_async_remote_copy(
        src_ref=src,
        dst_ref=dst,
        send_sem=send_sem,
        recv_sem=recv_sem,
        device_id={"head": head, "blk": blk},
        device_id_type=MESH,
    )


def greet(partners):
    barrier = pltpu.get_barrier_semaphore()
    for head, blk in partners:
        pl.semaphore_signal(
            barrier, inc=1, device_id={"head": head, "blk": blk}, device_id_type=MESH
        )
    pl.semaphore_wait(barrier, len(partners))


def xor(value, bit):
    return value + bit - 2 * bit * (lax.div(value, bit) % 2)


def partners_of(head, blk, nblk, heads=True, blks=True):
    found = []
    if heads:
        found += [(xor(head, 1), blk), (xor(head, 2), blk), (3 - head, blk)]
    if blks:
        found += [(head, lax.rem(blk + d, nblk)) for d in range(1, nblk)]
    return found


def front_kernel(
    nblk, pieces, tok, first, w_q, w_k, w_v, gains,
    tok_all, first_all, q_all, k_all, v_own, v_all, gain_all,
    own_sem, send_x, recv_x, send_s, recv_s, send_f, recv_f, send_w, recv_w, send_v, recv_v,
):
    head, blk = lax.axis_index("head"), lax.axis_index("blk")
    side, core, far = xor(head, 2), xor(head, 1), 3 - head
    greet(partners_of(head, blk, nblk))
    moved = [(tok, tok_all), (first, first_all)]
    weights = [(w_q, q_all), (w_k, k_all), (w_v, v_own), (gains, gain_all)]
    rows = tok.shape[0] // pieces

    def part(ref, p):
        return ref.at[pl.ds(p * rows, rows)]

    def hop(sems, k, p, source, slot, target):
        dst = part(moved[k][1].at[slot], p)
        return remote(source, dst, sems[0].at[k, p], sems[1].at[k, p], target, blk)

    xs, ss, fs = (send_x, recv_x), (send_s, recv_s), (send_f, recv_f)
    order = [(k, p) for p in range(pieces) for k in range(2)]
    for k, p in order:
        hop(xs, k, p, part(moved[k][0], p), head, side).start()

    def spread(d):
        to = lax.rem(blk + d, nblk)
        return [
            remote(src, dst.at[blk], send_w.at[i, d], recv_w.at[i, d], head, to)
            for i, (src, dst) in enumerate(weights)
        ]

    def from_peer(d):
        source = lax.rem(blk - d + nblk, nblk)
        return [
            remote(src, dst.at[source], send_w.at[i, d], recv_w.at[i, d], head, source)
            for i, (src, dst) in enumerate(weights)
        ]

    for d in range(1, nblk):
        for copy in spread(d):
            copy.start()
    for k, p in order:
        hop(ss, k, p, part(moved[k][0], p), head, core).start()
    local = [
        pltpu.make_async_copy(moved[k][0], moved[k][1].at[head], own_sem.at[k]) for k in range(2)
    ] + [
        pltpu.make_async_copy(src, dst.at[blk], own_sem.at[2 + i])
        for i, (src, dst) in enumerate(weights)
    ]
    for copy in local:
        copy.start()
    for k, p in order:
        landed = part(moved[k][1].at[side], p)
        hop(xs, k, p, landed, side, side).wait_recv()
        hop(fs, k, p, landed, side, core).start()
    for copy in local:
        copy.wait()
    for d in range(1, nblk):
        for copy in from_peer(d):
            copy.wait_recv()
    half, kind = lax.div(head, 2), lax.rem(head, 2)
    for i in range(2):
        target = half + 2 * i

        @pl.when(target == head)
        def _():
            pltpu.make_async_copy(v_own, v_all.at[kind], own_sem.at[6]).start()

        @pl.when(target != head)
        def _():
            remote(v_own, v_all.at[kind], send_v.at[i], recv_v.at[kind], target, blk).start()

    for k, p in order:
        hop(ss, k, p, part(moved[k][1].at[core], p), core, core).wait_recv()
        hop(fs, k, p, part(moved[k][1].at[far], p), far, core).wait_recv()
    for c in range(2):
        source = 2 * kind + c

        @pl.when(source == head)
        def _():
            pltpu.make_async_copy(v_own, v_all.at[c], own_sem.at[6]).wait()

        @pl.when(source != head)
        def _():
            remote(v_own, v_all.at[c], send_v.at[0], recv_v.at[c], source, blk).wait_recv()

    for i in range(2):
        target = half + 2 * i

        @pl.when(target != head)
        def _():
            remote(v_own, v_all.at[kind], send_v.at[i], recv_v.at[kind], target, blk).wait_send()

    for k, p in order:
        hop(xs, k, p, part(moved[k][0], p), head, side).wait_send()
        hop(ss, k, p, part(moved[k][0], p), head, core).wait_send()
        hop(fs, k, p, part(moved[k][1].at[side], p), side, core).wait_send()
    for d in range(1, nblk):
        for copy in spread(d):
            copy.wait_send()


def front(nblk, tok, first, w_q, w_k, w_v, gains, pieces=4):
    def shape(lead, like):
        return jax.ShapeDtypeStruct(lead + like.shape, like.dtype)

    dma = pltpu.SemaphoreType.DMA
    return pl.pallas_call(
        functools.partial(front_kernel, nblk, pieces),
        out_shape=[
            shape((4,), tok),
            shape((4,), first),
            shape((nblk,), w_q),
            shape((nblk,), w_k),
            shape((nblk,), w_v),
            shape((2, nblk), w_v),
            shape((nblk,), gains),
        ],
        in_specs=[ANY] * 6,
        out_specs=[ANY] * 7,
        scratch_shapes=[dma((7,))]
        + [dma((2, pieces))] * 6
        + [dma((4, nblk))] * 2
        + [dma((2,))] * 2,
        compiler_params=pltpu.CompilerParams(collective_id=0, has_side_effects=True),
        name="front",
    )(tok, first, w_q, w_k, w_v, gains)


def halo_kernel(nblk, pieces, own, near_far, send_z, recv_z, send_y, recv_y):
    head, blk = lax.axis_index("head"), lax.axis_index("blk")
    odd = lax.rem(blk, 2)
    pair = blk + 1 - 2 * odd
    up, down = lax.rem(blk + 2, nblk), lax.rem(blk + nblk - 2, nblk)
    barrier = pltpu.get_barrier_semaphore()
    for to in (pair, up, down):
        pl.semaphore_signal(
            barrier, inc=1, device_id={"head": head, "blk": to}, device_id_type=MESH
        )
    pl.semaphore_wait(barrier, 3)
    rows = own.shape[0] // pieces

    def part(ref, p):
        return ref.at[pl.ds(p * rows, rows)]

    def far_copy(p, to):
        return remote(part(own, p), part(near_far.at[0], p), send_z.at[p], recv_z.at[p], head, to)

    def near_copy(p, src):
        return remote(src, part(near_far.at[1], p), send_y.at[p], recv_y.at[p], head, pair)

    for p in range(pieces):

        @pl.when(blk + 2 < nblk)
        def _():
            far_copy(p, up).start()

        @pl.when(odd == 0)
        def _():
            near_copy(p, part(own, p)).start()

    for p in range(pieces):

        @pl.when(blk >= 2)
        def _():
            far_copy(p, down).wait_recv()

        @pl.when((blk >= 2) & (odd == 1))
        def _():
            near_copy(p, part(near_far.at[0], p)).start()

    for p in range(pieces):

        @pl.when((blk >= 2) | (odd == 1))
        def _():
            near_copy(p, part(own, p)).wait_recv()

        @pl.when(blk + 2 < nblk)
        def _():
            far_copy(p, up).wait_send()

        @pl.when((blk >= 2) | (odd == 0))
        def _():
            near_copy(p, part(own, p)).wait_send()


def halo(nblk, own, pieces=8):
    dma = pltpu.SemaphoreType.DMA
    return pl.pallas_call(
        functools.partial(halo_kernel, nblk, pieces),
        out_shape=jax.ShapeDtypeStruct((2,) + own.shape, own.dtype),
        in_specs=[ANY],
        out_specs=ANY,
        scratch_shapes=[dma((pieces,))] * 4,
        compiler_params=pltpu.CompilerParams(collective_id=1, has_side_effects=True),
        name="halo",
    )(own)


def swap_kernel(nblk, parts, out, own_sem, send_sem, recv_sem):
    head, blk = lax.axis_index("head"), lax.axis_index("blk")
    others = [xor(head, 2), 3 - head, xor(head, 1)]
    greet(partners_of(head, blk, nblk, blks=False))
    copies = [
        remote(parts.at[to], out.at[head], send_sem.at[i], recv_sem.at[i], to, blk)
        for i, to in enumerate(others)
    ]
    for copy in copies:
        copy.start()
    local = pltpu.make_async_copy(parts.at[head], out.at[head], own_sem)
    local.start()
    local.wait()
    for i, to in enumerate(others):
        remote(parts.at[to], out.at[to], send_sem.at[i], recv_sem.at[i], to, blk).wait_recv()
    for copy in copies:
        copy.wait_send()


def swap(nblk, parts, collective_id):
    dma = pltpu.SemaphoreType.DMA
    return pl.pallas_call(
        functools.partial(swap_kernel, nblk),
        out_shape=jax.ShapeDtypeStruct(parts.shape, parts.dtype),
        in_specs=[ANY],
        out_specs=ANY,
        scratch_shapes=[dma, dma((3,)), dma((3,))],
        compiler_params=pltpu.CompilerParams(
            collective_id=collective_id, has_side_effects=True
        ),
        name="swap%d" % collective_id,
    )(parts)


def tail_kernel(
    nblk, pieces, grad, d_q, d_k, d_v, first, gains,
    out_grad, out_q, out_k, out_v, out_first, out_gain,
    core_buf, side_out, side_buf, q_buf, k_buf, v_buf, v_sum, v_got, gain_buf, gain_sum, gain_got,
    own_sem, send_s, recv_s, send_x, recv_x, send_w, recv_w, send_v, recv_v, send_f, recv_f,
    send_g, recv_g,
):
    head, blk = lax.axis_index("head"), lax.axis_index("blk")
    side, core, far = xor(head, 2), xor(head, 1), 3 - head
    greet(partners_of(head, blk, nblk))
    rows = grad.shape[1] // pieces

    def part(ref, p):
        return ref.at[pl.ds(p * rows, rows)]

    def to_core(i, p, slot):
        return remote(
            part(grad.at[slot], p), part(core_buf.at[i], p), send_s.at[i, p], recv_s.at[i, p],
            core, blk,
        )

    def to_side(p):
        return remote(
            part(side_out, p), part(side_buf, p), send_x.at[p], recv_x.at[p], side, blk
        )

    for p in range(pieces):
        to_core(0, p, far).start()
    for p in range(pieces):
        to_core(1, p, core).start()
    half, kind = lax.div(head, 2), lax.rem(head, 2)
    weights = [(d_q, q_buf), (d_k, k_buf), (d_v.at[0], v_buf.at[0]), (d_v.at[1], v_buf.at[1]),
               (gains, gain_buf)]

    def spread(d):
        to = lax.rem(blk + d, nblk)
        return [
            remote(src.at[to], dst.at[blk], send_w.at[i, d], recv_w.at[i, d], head, to)
            for i, (src, dst) in enumerate(weights)
        ]

    def from_peer(d):
        source = lax.rem(blk - d + nblk, nblk)
        return [
            remote(src.at[source], dst.at[source], send_w.at[i, d], recv_w.at[i, d], head, source)
            for i, (src, dst) in enumerate(weights)
        ]

    for d in range(1, nblk):
        for copy in spread(d):
            copy.start()
    local = [
        pltpu.make_async_copy(src.at[blk], dst.at[blk], own_sem.at[i])
        for i, (src, dst) in enumerate(weights)
    ]
    for copy in local:
        copy.start()

    def first_copy(i, to, slot):
        return remote(first.at[to], out_first.at[slot], send_f.at[i], recv_f.at[slot], to, blk)

    @pl.when(half == 1)
    def _():
        for i, to in enumerate((core, side, far)):
            first_copy(i, to, kind).start()
        pltpu.make_async_copy(first.at[head], out_first.at[kind], own_sem.at[5]).start()

    for p in range(pieces):
        to_core(0, p, far).wait_recv()
        part(side_out, p)[...] = (
            part(grad.at[side], p)[...].astype(F32) + part(core_buf.at[0], p)[...].astype(F32)
        ).astype(BF16)
        to_side(p).start()
    for copy in local:
        copy.wait()
    for d in range(1, nblk):
        for copy in from_peer(d):
            copy.wait_recv()
    out_q[...] = jnp.sum(q_buf[...].astype(F32), axis=0)
    out_k[...] = jnp.sum(k_buf[...].astype(F32), axis=0)
    v_sum[...] = jnp.sum(v_buf[...].astype(F32), axis=1)
    gain_sum[...] = jnp.sum(gain_buf[...], axis=0)
    peers = (core, side, far)
    for i, to in enumerate(peers):
        remote(gain_sum, gain_got.at[i], send_g.at[i], recv_g.at[i], to, blk).start()

    def give(c, to):
        return remote(v_sum.at[c], v_got, send_v.at[c], recv_v.at[0], to, blk)

    for c in range(2):
        to = 2 * head + c

        @pl.when((half == 0) & (to != head))
        def _():
            give(c, to).start()

    for p in range(pieces):
        to_core(1, p, core).wait_recv()
        to_side(p).wait_recv()
        part(out_grad, p)[...] = (
            part(grad.at[head], p)[...].astype(F32)
            + part(core_buf.at[1], p)[...].astype(F32)
            + part(side_buf, p)[...].astype(F32)
        )
    for i, to in enumerate(peers):
        remote(gain_sum, gain_got.at[i], send_g.at[i], recv_g.at[i], to, blk).wait_recv()
    out_gain[...] = gain_sum[...] + gain_got[0] + gain_got[1] + gain_got[2]

    @pl.when(head == 0)
    def _():
        out_v[...] = v_sum[0]

    @pl.when(head != 0)
    def _():
        give(0, half).wait_recv()
        out_v[...] = v_got[...]

    for slot in range(2):

        @pl.when(head == 2 + slot)
        def _():
            pltpu.make_async_copy(first.at[head], out_first.at[slot], own_sem.at[5]).wait()

        @pl.when(head != 2 + slot)
        def _():
            first_copy(0, 2 + slot, slot).wait_recv()

    @pl.when(half == 1)
    def _():
        for i, to in enumerate((core, side, far)):
            first_copy(i, to, kind).wait_send()

    for c in range(2):
        to = 2 * head + c

        @pl.when((half == 0) & (to != head))
        def _():
            give(c, to).wait_send()

    for i, to in enumerate(peers):
        remote(gain_sum, gain_got.at[i], send_g.at[i], recv_g.at[i], to, blk).wait_send()
    for p in range(pieces):
        to_core(0, p, far).wait_send()
        to_core(1, p, core).wait_send()
        to_side(p).wait_send()
    for d in range(1, nblk):
        for copy in spread(d):
            copy.wait_send()


def tail(nblk, grad, d_q, d_k, d_v, first, gains, pieces=4):
    dma = pltpu.SemaphoreType.DMA
    row, half = grad.shape[1:], d_v.shape[2:]
    piece = (2, pieces)
    return pl.pallas_call(
        functools.partial(tail_kernel, nblk, pieces),
        out_shape=[
            jax.ShapeDtypeStruct(row, F32),
            jax.ShapeDtypeStruct(d_q.shape[1:], F32),
            jax.ShapeDtypeStruct(d_k.shape[1:], F32),
            jax.ShapeDtypeStruct(half, F32),
            jax.ShapeDtypeStruct((2,) + first.shape[1:], BF16),
            jax.ShapeDtypeStruct(gains.shape[1:], F32),
        ],
        in_specs=[WHOLE] * 6,
        out_specs=[WHOLE] * 6,
        scratch_shapes=[
            pltpu.VMEM((2,) + row, BF16),
            pltpu.VMEM(row, BF16),
            pltpu.VMEM(row, BF16),
            pltpu.VMEM(d_q.shape, BF16),
            pltpu.VMEM(d_k.shape, BF16),
            pltpu.VMEM((2, nblk) + half, BF16),
            pltpu.VMEM((2,) + half, F32),
            pltpu.VMEM(half, F32),
            pltpu.VMEM(gains.shape, F32),
            pltpu.VMEM(gains.shape[1:], F32),
            pltpu.VMEM((3,) + gains.shape[1:], F32),
            dma((6,)),
            dma(piece), dma(piece),
            dma((pieces,)), dma((pieces,)),
            dma((5, nblk)), dma((5, nblk)),
            dma((2,)), dma((1,)),
            dma((3,)), dma((2,)),
            dma((3,)), dma((3,)),
        ],
        compiler_params=pltpu.CompilerParams(
            collective_id=4, has_side_effects=True, vmem_limit_bytes=48 << 20
        ),
        name="tail",
    )(grad, d_q, d_k, d_v, first, gains)


def head_mask(rows, h, heads, width, dtype=BF16):
    lane=lax.broadcasted_iota(jnp.int32,(rows,width),1)
    real=heads*HEAD_DIM
    m=((lane>=h*HEAD_DIM)&(lane<(h+1)*HEAD_DIM))|((lane>=real+3*h)&(lane<real+3*h+3))
    return m

def doc_start(meta, ndocs, t):
    def step(j,c):
        cum,best=c
        best=jnp.where(cum<=t,cum,best)
        return cum+meta[1+j],best
    return lax.fori_loop(0,ndocs,step,(jnp.int32(0),jnp.int32(0)))[1]

def doc_end(meta, ndocs, t):
    def step(j,c):
        cum,best,found=c
        cum=cum+meta[1+j]
        take=(cum>t)&(found==0)
        return cum,jnp.where(take,cum,best),jnp.where(take,1,found)
    return lax.fori_loop(0,ndocs,step,(jnp.int32(0),jnp.int32(0),jnp.int32(0)))[1]

def starts_vec(meta, ndocs, t):
    def step(j,c):
        cum,best=c
        return cum+meta[1+j],jnp.where(cum<=t,cum,best)
    return lax.fori_loop(0,ndocs,step,(jnp.int32(0),jnp.zeros(t.shape,jnp.int32)))[1]

def ends_vec(meta, ndocs, t):
    def step(j,c):
        cum,best=c
        ln=meta[1+j]
        return cum+ln,jnp.where(cum<=t,cum+ln,best)
    return lax.fori_loop(0,ndocs,step,(jnp.int32(0),jnp.zeros(t.shape,jnp.int32)))[1]

def three(lo,a,b,hi,body):
    lax.fori_loop(lo,a,lambda j,_: body(j,True),None)
    lax.fori_loop(a,b,lambda j,_: body(j,False),None)
    lax.fori_loop(b,hi,lambda j,_: body(j,True),None)

def fwd_kernel(heads,ndocs,tq,tk,reach, meta, q_ref,k_ref,v_ref,mix_ref,o32_ref,qaug_ref, qh, m_ref, acc_ref):
    i=pl.program_id(0)
    width=q_ref.shape[1]; real=heads*HEAD_DIM
    base=meta[0]; wbase=base-reach
    t0=base+i*tq
    lo=(doc_start(meta,ndocs,t0)-wbase)//tk
    f0=(doc_start(meta,ndocs,t0+tq-1)-wbase+tk-1)//tk
    f1=(t0-wbase)//tk
    hi=(t0+tq-1-wbase)//tk+1
    f0=jnp.minimum(f0,f1)
    q=q_ref[...]
    for h in range(heads):
        qh[h]=jnp.where(head_mask(tq,h,heads,width),q,jnp.zeros_like(q))
        m_ref[h]=jnp.full((tq,128),EXCLUDED,F32)
    acc_ref[...]=jnp.zeros_like(acc_ref)
    trow=t0+lax.broadcasted_iota(jnp.int32,(tq,128),0)
    srow=starts_vec(meta,ndocs,trow)
    lane=lax.broadcasted_iota(jnp.int32,(tq,width),1)
    def body(j,masked):
        off=pl.multiple_of(j*tk,tk)
        k=k_ref[pl.ds(off,tk),:]; v=v_ref[pl.ds(off,tk),:]
        if masked:
            u=wbase+off+lax.broadcasted_iota(jnp.int32,(tq,tk),1)
            vis=(u>=srow[:,:1])&(u<=trow[:,:1])
        pv=None; scale=None
        for h in range(heads):
            s=dotf(qh[h],k,NT)
            if masked: s=jnp.where(vis,s,EXCLUDED)
            mp=m_ref[h][:,:1]
            mn=jnp.maximum(mp,jnp.max(s,axis=1,keepdims=True))
            al=jnp.exp(mp-mn)
            p=jnp.exp(s-mn).astype(BF16)
            m_ref[h]=jnp.broadcast_to(mn,(tq,128))
            vh=jnp.where(head_mask(tk,h,heads,width),v,jnp.zeros_like(v))
            d=dotf(p,vh)
            pv=d if pv is None else pv+d
            scale=jnp.broadcast_to(al,(tq,width)) if scale is None else jnp.where(head_mask(tq,h,heads,width),al,scale)
        acc_ref[...]=acc_ref[...]*scale+pv
    three(lo,f0,f1,hi,body)
    acc=acc_ref[...]
    out=jnp.zeros((tq,width),F32); aug=q.astype(F32)
    for h in range(heads):
        l=acc[:,real+3*h:real+3*h+1]
        out=jnp.where(head_mask(tq,h,heads,width),acc/l,out)
        neg=-(m_ref[h][:,:1]+jnp.log(l))
        c0=neg.astype(BF16).astype(F32)
        c1=(neg-c0).astype(BF16).astype(F32)
        c2=neg-c0-c1
        aug=jnp.where(lane==real+3*h,c0,jnp.where(lane==real+3*h+1,c1,jnp.where(lane==real+3*h+2,c2,aug)))
    mix_ref[...]=out[:,:real].astype(BF16)
    o32_ref[...]=out
    qaug_ref[...]=aug.astype(BF16)

def attention_fwd(meta,q,k,v,heads,tq=256,tk=512):
    B,width=q.shape; W=k.shape[0]; ndocs=meta.shape[0]-1
    full=lambda: pl.BlockSpec((W,width),lambda i:(0,0),pipeline_mode=pl.Buffered(1))
    row=lambda w: pl.BlockSpec((tq,w),lambda i:(i,0))
    return pl.pallas_call(functools.partial(fwd_kernel,heads,ndocs,tq,tk,W-B),
        grid=(B//tq,),
        in_specs=[pl.BlockSpec(memory_space=pltpu.SMEM),row(width),full(),full()],
        out_specs=[row(heads*HEAD_DIM),row(width),row(width)],
        out_shape=[jax.ShapeDtypeStruct((B,heads*HEAD_DIM),BF16),jax.ShapeDtypeStruct((B,width),F32),jax.ShapeDtypeStruct((B,width),BF16)],
        scratch_shapes=[pltpu.VMEM((heads,tq,width),BF16),pltpu.VMEM((heads,tq,128),F32),pltpu.VMEM((tq,width),F32)],
        compiler_params=pltpu.CompilerParams(vmem_limit_bytes=56<<20),
        cost_estimate=pl.CostEstimate(flops=30_000_000_000,bytes_accessed=12<<20,transcendentals=20_000_000),
        name="attn_fwd")(meta,q,k,v)

def dq_kernel(heads,ndocs,tq,tk,reach, meta, q_ref,do_ref,k_ref,v_ref,dq_ref, qh, doh, acc_ref):
    i=pl.program_id(0)
    width=q_ref.shape[1]; real=heads*HEAD_DIM
    base=meta[0]; wbase=base-reach
    t0=base+i*tq
    lo=(doc_start(meta,ndocs,t0)-wbase)//tk
    f0=(doc_start(meta,ndocs,t0+tq-1)-wbase+tk-1)//tk
    f1=(t0-wbase)//tk
    hi=(t0+tq-1-wbase)//tk+1
    f0=jnp.minimum(f0,f1)
    q=q_ref[...]; do=do_ref[...]
    for h in range(heads):
        hm=head_mask(tq,h,heads,width)
        qh[h]=jnp.where(hm,q,jnp.zeros_like(q))
        doh[h]=jnp.where(hm,do,jnp.zeros_like(do))
    acc_ref[...]=jnp.zeros_like(acc_ref)
    trow=t0+lax.broadcasted_iota(jnp.int32,(tq,128),0)
    srow=starts_vec(meta,ndocs,trow)
    def body(j,masked):
        off=pl.multiple_of(j*tk,tk)
        k=k_ref[pl.ds(off,tk),:]; v=v_ref[pl.ds(off,tk),:]
        if masked:
            u=wbase+off+lax.broadcasted_iota(jnp.int32,(tq,tk),1)
            vis=(u>=srow[:,:1])&(u<=trow[:,:1])
        tot=None
        for h in range(heads):
            p=jnp.exp(dotf(qh[h],k,NT))
            if masked: p=jnp.where(vis,p,0.0)
            ds=(p*dotf(doh[h],v,NT)).astype(BF16)
            kh=jnp.where(head_mask(tk,h,heads,width),k,jnp.zeros_like(k))
            d=dotf(ds,kh)
            tot=d if tot is None else tot+d
        acc_ref[...]+=tot
    three(lo,f0,f1,hi,body)
    dq_ref[...]=(acc_ref[...]*(HEAD_DIM**-0.5)).astype(BF16)[:,:real]

def attention_dq(meta,q,do,k,v,heads,tq=256,tk=512):
    B,width=q.shape; W=k.shape[0]; ndocs=meta.shape[0]-1
    full=lambda: pl.BlockSpec((W,width),lambda i:(0,0),pipeline_mode=pl.Buffered(1))
    row=lambda w: pl.BlockSpec((tq,w),lambda i:(i,0))
    return pl.pallas_call(functools.partial(dq_kernel,heads,ndocs,tq,tk,W-B),
        grid=(B//tq,),
        in_specs=[pl.BlockSpec(memory_space=pltpu.SMEM),row(width),row(width),full(),full()],
        out_specs=row(heads*HEAD_DIM),
        out_shape=jax.ShapeDtypeStruct((B,heads*HEAD_DIM),BF16),
        scratch_shapes=[pltpu.VMEM((heads,tq,width),BF16)]*2+[pltpu.VMEM((tq,width),F32)],
        compiler_params=pltpu.CompilerParams(vmem_limit_bytes=56<<20),
        cost_estimate=pl.CostEstimate(flops=45_000_000_000,bytes_accessed=12<<20,transcendentals=20_000_000),
        name="attn_dq")(meta,q,do,k,v)

def dkv_kernel(heads,ndocs,tq,tk,meta, k_ref,v_ref,q_ref,do_ref,dk_ref,dv_ref, kh, vh, dk_acc, dv_acc):
    i=pl.program_id(0)
    width=k_ref.shape[1]; real=heads*HEAD_DIM
    base=meta[0]
    u0=base+i*tk
    lo=(u0-base)//tq
    f0=(u0+tk-1-base+tq-1)//tq
    e_first=doc_end(meta,ndocs,u0); e_last=doc_end(meta,ndocs,u0+tk-1)
    f1=(e_first-base)//tq
    hi=(e_last-1-base)//tq+1
    f0=jnp.minimum(f0,hi)
    f1=jnp.clip(f1,f0,hi)
    k=k_ref[...]; v=v_ref[...]
    for h in range(heads):
        hm=head_mask(tk,h,heads,width)
        kh[h]=jnp.where(hm,k,jnp.zeros_like(k))
        vh[h]=jnp.where(hm,v,jnp.zeros_like(v))
    dk_acc[...]=jnp.zeros_like(dk_acc); dv_acc[...]=jnp.zeros_like(dv_acc)
    urow=u0+lax.broadcasted_iota(jnp.int32,(tk,128),0)
    erow=ends_vec(meta,ndocs,urow)
    def body(j,masked):
        off=pl.multiple_of(j*tq,tq)
        q=q_ref[pl.ds(off,tq),:]; do=do_ref[pl.ds(off,tq),:]
        if masked:
            t=base+off+lax.broadcasted_iota(jnp.int32,(tk,tq),1)
            vis=(t>=urow[:,:1])&(t<erow[:,:1])
        a=None;b=None
        for h in range(heads):
            p=jnp.exp(dotf(kh[h],q,NT))
            if masked: p=jnp.where(vis,p,0.0)
            ds=(p*dotf(vh[h],do,NT)).astype(BF16)
            hm=head_mask(tq,h,heads,width)
            d=dotf(p.astype(BF16),jnp.where(hm,do,jnp.zeros_like(do)))
            a=d if a is None else a+d
            d=dotf(ds,jnp.where(hm,q,jnp.zeros_like(q)))
            b=d if b is None else b+d
        dv_acc[...]+=a
        dk_acc[...]+=b
    three(lo,f0,f1,hi,body)
    dk_ref[...]=dk_acc[...].astype(BF16)[:,:real]
    dv_ref[...]=dv_acc[...].astype(BF16)[:,:real]

def attention_dkv(meta,k,v,q,do,heads,tq=512,tk=256):
    B,width=k.shape; W=q.shape[0]; ndocs=meta.shape[0]-1
    full=lambda: pl.BlockSpec((W,width),lambda i:(0,0),pipeline_mode=pl.Buffered(1))
    row=lambda w: pl.BlockSpec((tk,w),lambda i:(i,0))
    return pl.pallas_call(functools.partial(dkv_kernel,heads,ndocs,tq,tk),
        grid=(B//tk,),
        in_specs=[pl.BlockSpec(memory_space=pltpu.SMEM),row(width),row(width),full(),full()],
        out_specs=[row(heads*HEAD_DIM)]*2,
        out_shape=[jax.ShapeDtypeStruct((B,heads*HEAD_DIM),BF16)]*2,
        scratch_shapes=[pltpu.VMEM((heads,tk,width),BF16)]*2+[pltpu.VMEM((tk,width),F32)]*2,
        compiler_params=pltpu.CompilerParams(vmem_limit_bytes=56<<20),
        cost_estimate=pl.CostEstimate(flops=60_000_000_000,bytes_accessed=12<<20,transcendentals=20_000_000),
        name="attn_dkv")(meta,k,v,q,do)


def statistics(values):
    center = values - jnp.mean(values, axis=-1, keepdims=True)
    scale = lax.rsqrt(jnp.mean(jnp.square(center), axis=-1, keepdims=True) + EPSILON)
    return center * scale, scale


def norm_back(grad, xhat, scale, gain):
    eg = grad * gain
    return scale * (
        eg
        - jnp.mean(eg, axis=-1, keepdims=True)
        - xhat * jnp.mean(eg * xhat, axis=-1, keepdims=True)
    )


def gelu_tanh(values):
    return (
        0.5 * values * (1.0 + jnp.tanh(GELU_SCALE * (values + 0.044715 * values * values * values)))
    )


def split_parts(values):
    high = values.astype(BF16)
    rest = values - high.astype(F32)
    middle = rest.astype(BF16)
    return high, middle, (rest - middle.astype(F32)).astype(BF16)


def widened(columns, extra):
    rows, width = columns.shape
    empty = jnp.zeros((rows, WIDTH - width - extra.shape[1]), BF16)
    return jnp.concatenate([columns, extra, empty], axis=1)


def on_device(
    tokens, first_values, cotangent, w_query, w_key, w_value, w_out, w_up, w_down,
    gain_attn, gain_mlp, doc_lengths,
):
    width = tokens.shape[1]
    heads_of = lax.axis_size("head")
    nblk = lax.axis_size("blk")
    head, blk = lax.axis_index("head"), lax.axis_index("blk")
    rows = tokens.shape[0]
    block = rows * heads_of
    heads = HEADS // heads_of
    cols = heads * HEAD_DIM
    part = width // nblk
    scale = HEAD_DIM**-0.5
    both = ("blk", "head")
    meta = jnp.concatenate([jnp.reshape(blk * block, (1,)).astype(jnp.int32), doc_lengths])

    packed = jnp.concatenate([w_up, w_down.T, w_out.T], axis=1)
    gathered = lax.all_gather(packed, both, axis=0).reshape(nblk, heads_of, part, packed.shape[1])

    def unpacked(lo, hi):
        return gathered[:, :, :, lo:hi].transpose(0, 2, 1, 3).reshape(width, heads_of * (hi - lo))

    up_cols = w_up.shape[1]
    full_up, down_t = unpacked(0, up_cols), unpacked(up_cols, 2 * up_cols)
    out_t = unpacked(2 * up_cols, packed.shape[1])

    gains = jnp.stack([gain_attn, gain_mlp])[:, None, :]
    tok_all, first_all, q_all, k_all, _, v_all, gain_all = front(
        nblk, tokens, first_values, w_query, w_key, w_value, gains
    )
    attn_gain = gain_all[:, 0].reshape(width)
    mlp_gain = gain_all[:, 1].reshape(width)
    wq, wk = q_all.reshape(width, cols), k_all.reshape(width, cols)
    v_halves = v_all.reshape(2, width, w_value.shape[1])
    wv = jnp.concatenate([v_halves[0], v_halves[1]], axis=1)
    xhat_all, _ = statistics(tok_all.reshape(block, width).astype(F32))
    normed = (xhat_all * attn_gain).astype(BF16)
    query = (dotf(normed, wq).astype(BF16).astype(F32) * scale).astype(BF16)
    key = dotf(normed, wk).astype(BF16)
    fresh = dotf(normed, wv).astype(BF16)
    kept = lax.dynamic_slice_in_dim(
        first_all.reshape(block, first_values.shape[1]), cols * (head % 2), cols, 1
    )
    value = jnp.where(head < 2, fresh, kept)

    pair = 2 * HEAD_DIM
    sent = jnp.concatenate([key[:, :pair], value[:, :pair], key[:, pair:], value[:, pair:]], axis=1)
    earlier = halo(nblk, sent)
    window = jnp.concatenate([earlier[0], earlier[1], sent], axis=0)
    ones = jnp.ones((window.shape[0], SPLITS * heads), BF16)
    key_win = widened(
        jnp.concatenate([window[:, :pair], window[:, 2 * pair : 2 * pair + HEAD_DIM]], axis=1), ones
    )
    value_win = widened(
        jnp.concatenate([window[:, pair : 2 * pair], window[:, 2 * pair + HEAD_DIM :]], axis=1), ones
    )
    no_extra = jnp.zeros((block, SPLITS * heads), BF16)
    mixed_heads, exact, query_wide = attention_fwd(
        meta, widened(query, no_extra), key_win, value_win, heads, 512, 1024
    )

    mixed = swap(nblk, mixed_heads.reshape(heads_of, rows, cols), 2)
    mixed = mixed.transpose(1, 0, 2).reshape(rows, width)
    token_f = tokens.astype(F32)
    resid = token_f + dotf(mixed, out_t, NT)
    xhat2, scale2 = statistics(resid)
    normed2 = (xhat2 * mlp_gain).astype(BF16)
    pre = dotf(normed2, full_up)
    hidden, gelu_back = jax.vjp(gelu_tanh, pre)
    hidden = hidden.astype(BF16)
    layer_output = (resid + dotf(hidden, down_t, NT)).astype(BF16)
    grad_hidden = dotf(cotangent, down_t)
    grad_pre = gelu_back(grad_hidden)[0].astype(BF16)
    grad_normed2 = dotf(grad_pre, full_up, NT)
    grad_resid = cotangent.astype(F32) + norm_back(grad_normed2, xhat2, scale2, mlp_gain)
    grad_branch = grad_resid.astype(BF16)
    grad_mixed = dotf(grad_branch, out_t).astype(BF16)
    grad_heads = swap(
        nblk, grad_mixed.reshape(rows, heads_of, cols).transpose(1, 0, 2), 3
    ).reshape(block, cols)

    gain_mlp_part = jnp.sum(grad_normed2 * xhat2, axis=0)
    whole_up = dotf(normed2, grad_pre, TN)
    whole_down = dotf(cotangent, hidden, TN)
    whole_out = dotf(grad_branch, mixed, TN)

    def repacked(whole):
        return (
            whole.astype(BF16)
            .reshape(nblk, part, heads_of, whole.shape[1] // heads_of)
            .transpose(0, 2, 1, 3)
        )

    grads = jnp.concatenate([repacked(whole_up), repacked(whole_down), repacked(whole_out)], axis=3)
    grads = grads.reshape(nblk * heads_of, part, packed.shape[1])
    reduced = lax.psum_scatter(grads, both, scatter_dimension=0, tiled=False).astype(F32)

    delta = jnp.sum(
        (grad_heads.astype(F32) * exact[:, :cols]).reshape(block, heads, HEAD_DIM), axis=2
    )
    delta_parts = jnp.stack(split_parts(-delta), axis=2).reshape(block, SPLITS * heads)
    grad_wide = widened(grad_heads, delta_parts)

    def from_later(array, distance):
        route = [(i, i - distance) for i in range(distance, nblk)]
        return lax.ppermute(array, "blk", route)

    def later_window(array):
        return jnp.concatenate([array, from_later(array, 1), from_later(array, 2)], axis=0)

    query_later, grad_later = later_window(query_wide), later_window(grad_wide)
    grad_query = attention_dq(meta, query_wide, grad_wide, key_win, value_win, heads, 512, 512)
    own = key_win.shape[0] - block
    grad_key, grad_value = attention_dkv(
        meta, key_win[own:], value_win[own:], query_later, grad_later, heads, 512, 512
    )

    whole_q, whole_k, whole_v = (
        dotf(normed, grad_query, TN),
        dotf(normed, grad_key, TN),
        dotf(normed, grad_value, TN),
    )
    fresh_grad = jnp.where(head < 2, grad_value, jnp.zeros_like(grad_value))
    grad_normed = dotf(grad_query, wq, NT) + dotf(grad_key, wk, NT) + dotf(fresh_grad, wv, NT)
    gain_attn_part = jnp.sum(grad_normed * xhat_all, axis=0)
    gain_parts = jnp.stack([gain_attn_part, gain_mlp_part]).reshape(2, nblk, 1, part)
    v_parts = whole_v.astype(BF16).reshape(nblk, part, 2, cols // 2).transpose(2, 0, 1, 3)
    grad_norm_sum, final_query, final_key, final_value, first_parts, gain_sums = tail(
        nblk,
        grad_normed.astype(BF16).reshape(heads_of, rows, width),
        whole_q.astype(BF16).reshape(nblk, part, cols),
        whole_k.astype(BF16).reshape(nblk, part, cols),
        v_parts,
        grad_value.reshape(heads_of, rows, cols),
        gain_parts.transpose(1, 0, 2, 3),
    )
    xhat, scale1 = statistics(token_f)
    grad_tokens = grad_resid + norm_back(grad_norm_sum, xhat, scale1, attn_gain)
    grad_first = jnp.concatenate([first_parts[0], first_parts[1]], axis=1).astype(F32)
    return (
        layer_output,
        grad_tokens,
        grad_first,
        final_query,
        final_key,
        final_value,
        reduced[:, 2 * up_cols :].T,
        reduced[:, :up_cols],
        reduced[:, up_cols : 2 * up_cols].T,
        gain_sums[0].reshape(part),
        gain_sums[1].reshape(part),
    )


def solution(mesh):
    rows = P(("blk", "head"), None)
    specs = (P("blk", "head"),) * 3 + (P("head", "blk"), P("blk", "head"), P("head", "blk"))
    gains = (P("blk"), P("blk"))
    return jax.shard_map(
        on_device,
        mesh=mesh,
        in_specs=(rows,) * 3 + specs + gains + (P(),),
        out_specs=(rows,) * 3 + specs + gains,
        check_vma=False,
    )
```

time: 1680 us -> 627 us (0.37)
  waiting for transfers between devices: 562 us -> 44.6 us
  matrix products: 578 us -> 64.6 us
  Pallas kernels: 0 us -> 326 us
  blocking collectives: 233 us -> 0 us
  loops' own time: 56.1 us -> 0 us
  other arithmetic: 101 us -> 68.8 us
  starting transfers between devices: 28.4 us -> 5.22 us
    dot_general x99 -> x18, matrix products: 578 us -> 64.6 us  [dotf(): return lax.dot_general(left, right, dims, preferred_element_type=F32)]
    pallas_call x0 -> x8, Pallas kernels: none -> 326 us  [the longest x1 85.3 us: tail(): pl.pallas_call(functools.partial(tail_kernel, nblk, pieces), out_shape=[j...]
    unnamed x24 -> x2, waiting for transfers between devices: 270 us -> 0.03 us
    reduce_scatter x7 -> x1, waiting for transfers between devices: 196 us -> 0.01 us  [on_device(): lax.psum_scatter(grads, both, scatter_dimension=0, tiled=False).astype(F32)]
    all_gather x5 -> x0, blocking collectives: 138 us -> none  [the longest x1 33.2 us: on_device(): lax.all_gather(w_key, 'blk', axis=0, tiled=True)]
    another operation x3 -> x0, loops' own time: 56.1 us -> none  [the longest x1 34.2 us: on_device(): lax.scan(back_hop, (last_query, jnp.stack([last_key, last_value])), (jnp....]
    unnamed x3 -> x0, blocking collectives: 53.4 us -> none
    all_to_all x3 -> x0, blocking collectives: 42.2 us -> none  [the longest x1 14.1 us: on_device(): lax.all_to_all(grad_q_heads, 'head', split_axis=0, concat_axis=1, tiled=T...]
  transfers between devices with their start and end apart: 28 -> 6, of which waited for: 16 -> 1; matrix products, arithmetic and copies ran while one was open for 38% -> 25% of each run, Pallas kernels for 0% -> 50%
where the time goes in v1:
time: 627 us; the launch traced here: 621 us
  Pallas kernels  326 us (52%)
  local copies, waits for them, and re-layouts  96 us (15%)
  other arithmetic  68.8 us (11%)
  matrix products  64.6 us (10%)
  waiting for transfers between devices  44.6 us (7%)
  between operations  15.2 us (2%)
    pallas_call x1, Pallas kernels, tail(): pl.pallas_call(functools.partial(tail_kernel, nblk, pieces), out_shape=[j...  85.3 us
    dot_general x18, matrix products, dotf(): return lax.dot_general(left, right, dims, preferred_element_type=F32)  64.6 us
    pallas_call x1, Pallas kernels, front(): pl.pallas_call(functools.partial(front_kernel, nblk, pieces), out_shape=[...  55.6 us
    pallas_call x1, Pallas kernels, halo(): pl.pallas_call(functools.partial(halo_kernel, nblk, pieces), out_shape=ja...  55.6 us
    pallas_call x1, Pallas kernels, attention_dkv(): pl.pallas_call(functools.partial(dkv_kernel, heads, ndocs, tq, tk), grid=...  51 us
    ppermute x4, waiting for transfers between devices, from_later(): return lax.ppermute(array, 'blk', route)  44.6 us
    pallas_call x1, Pallas kernels, attention_fwd(): pl.pallas_call(functools.partial(fwd_kernel, heads, ndocs, tq, tk, W - B)...  30.6 us
    pallas_call x2, Pallas kernels, swap(): pl.pallas_call(functools.partial(swap_kernel, nblk), out_shape=jax.ShapeD...  28.3 us
  transfers between devices with their start and end apart: 6, of which 1 were waited for; matrix products, arithmetic and copies ran while one was open for 25% of the time, Pallas kernels for 50%

profile of v1, /device:TPU:0, one launch (start us, length us, event | category | flops | bytes accessed | tf_op | source)
XLA Modules:
  0.0 620.8 jit_solution(13846365668958376970)
XLA Ops:
  8.1 1.8 pad_maximum_fusion.7
  11.2 55.6 %front.1 = (bf16[4,512,768]{2,1,0:T(8,128)(2,1)}, bf16[4,512,384]{2,1,0:T(8,128)(2,1)}, bf16[8,96,192]{2,1,0:T(8,128)(2,1)}, bf16[8,96,192]{2,1,0:T(8,128)(2,1)}...) custom-call(bf16[512,768]{1,0:T(8,128)(2,1)} %tok.1, ...), custom_call_target="tpu_custom_call" | custom-call | tf_op jit(solution)/shard_map/front/pallas_call | solution.py:173
  67.8 2.5 convert_reduce_fusion
  73.2 2.0 multiply_convert_fusion.1
  81.9 3.5 convolution_convert_fusion.4
  86.7 1.5 pad_maximum_fusion.3.own
  88.2 55.6 %halo.1 = bf16[2,2048,384]{2,1,0:T(8,128)(2,1)} custom-call(bf16[2048,384]{1,0:T(8,128)(2,1)} %pad_maximum_fusion.3.own), custom_call_target="tpu_custom_call" | custom-call | tf_op jit(solution)/shard_map/halo/pallas_call | solution.py:254
  150.0 17.5 %maximum_maximum_fusion = bf16[6144,384]{1,0:T(8,128)(2,1)S(1)} fusion(bf16[2048,64]{1,0:T(8,128)(2,1)S(1)} %copy-done.17, bf16[2048,64]{1,0:T(8,128)(2,1)S(1)} %copy-done.21, bf16[2048,128]{1,0:T(8,128)(2,1)S(1)} %copy-done.19, bf16[2048,128]{1,0:T(8,128)(2,1)S(1)} %copy-done.23, bf16[2048,384]{1,0:T(8,128)(2,1)S(1)} %get-tuple-element.105, ...), kind=kLoop, calls=%fused_computation.27 | loop fusion | flops 28311552 | bytes 9437184 | tf_op jit(solution)/shard_map/concatenate | solution.py:788
  168.5 3.5 maximum_maximum_fusion.2
  172.0 30.6 %attn_fwd.1 = (bf16[2048,192]{1,0:T(8,128)(2,1)}, f32[2048,256]{1,0:T(8,128)}, bf16[2048,256]{1,0:T(8,128)(2,1)}) custom-call(s32[17]{0:T(128)} %pad_add_fusion.meta, bf16[2048,256]{1,0:T(8,128)(2,1)} %pad_maximum_fusion.5.q_ref, bf16[6144,256]{1,0:T(8,128)(2,1)} %get-tuple-element.121.k_ref, bf16[6144,256]{1,0:T(8,128)(2,1)} %get-tuple-element.120.v_ref), custom_call_target="tpu_custom_call" | custom-call | flops 30000001024 | bytes 12582912 | tf_op jit(solution)/shard_map/attn_fwd/pallas_call | solution.py:588
  205.2 2.4 slice.121.k_ref
  207.6 2.3 slice.122.v_ref
  209.9 14.2 %swap2.1 = bf16[4,512,192]{2,1,0:T(8,128)(2,1)} custom-call(bf16[4,512,192]{2,1,0:T(8,128)(2,1)} %bitcast.169), custom_call_target="tpu_custom_call" | custom-call | tf_op jit(solution)/shard_map/swap2/pallas_call | solution.py:286
  226.8 44.6 %collective-permute-done.1 = bf16[2048,256]{1,0:T(8,128)(2,1)} collective-permute-done((bf16[2048,256]{1,0:T(8,128)(2,1)}, bf16[2048,256]{1,0:T(8,128)(2,1)}, u32[]{:S(2)}, u32[]{:S(2)}) %collective-permute-start.1) | collective-permute-done | bytes 1048608 | tf_op jit(solution)/shard_map/ppermute | solution.py:845
  271.4 3.1 pad_maximum_fusion.1.q_ref
  274.5 1.6 slice.118
  276.1 8.2 %fusion.34 = (bf16[8,4,96,768]{3,2,1,0:T(8,128)(2,1)}, bf16[8,4,96,768]{3,2,1,0:T(8,128)(2,1)}) fusion(bf16[8,4,96,1728]{3,2,1,0:T(8,128)(2,1)} %bitcast.154), kind=kLoop, calls=%fused_computation.112 | loop fusion | bytes 18874368 | tf_op jit(solution)/shard_map/slice | solution.py:760
  284.2 1.8 copy.95
  286.0 3.3 reshape.256
  289.4 6.4 %copy.97 = bf16[8,4,96,768]{3,1,2,0:T(4,128)(2,1)S(1)} copy(bf16[8,4,96,768]{3,2,1,0:T(8,128)(2,1)} %get-tuple-element.97) | data formatting | bytes 9437184
  298.9 3.6 copy.96
  304.9 2.9 fusion.33
  307.8 7.3 %fusion.3 = bf16[512,3072]{1,0:T(8,128)(2,1)S(1)} fusion(f32[512,3072]{1,0:T(8,128)S(1)} %fusion.33, bf16[512,768]{1,0:T(8,128)(2,1)S(1)} %copy-done.36, bf16[768,3072]{1,0:T(8,128)(2,1)S(1)} %bitcast.158), kind=kOutput, calls=%fused_computation.8 | convolution fusion | flops 2453667840 | bytes 14942208 | tf_op jit(solution)/shard_map/dot_general | solution.py:30
  315.1 3.5 multiply_reduce_fusion.2
  322.4 14.2 %swap3.1 = bf16[4,512,192]{2,1,0:T(8,128)(2,1)} custom-call(bf16[4,512,192]{2,1,0:T(8,128)(2,1)} %bitcast.163), custom_call_target="tpu_custom_call" | custom-call | tf_op jit(solution)/shard_map/swap3/pallas_call | solution.py:286
  336.5 3.4 slice_multiply_fusion
  339.9 2.9 copy.83
  345.6 2.7 pad_maximum_fusion.4.do_ref
  350.8 1.9 convolution_convert_fusion.5
  352.7 8.4 %fusion.10 = bf16[768,3072]{0,1:T(8,128)(2,1)} fusion(bf16[512,768]{1,0:T(8,128)(2,1)S(1)} %copy-done.37, f32[512,3072]{1,0:T(8,128)} %copy-done.56), kind=kOutput, calls=%fused_computation.28 | convolution fusion | flops 2432434176 | bytes 11796480 | tf_op jit(solution)/shard_map/dot_general | solution.py:30
  361.1 4.8 convolution_convert_fusion.1
  365.9 4.4 reshape.270
  370.3 6.6 %copy.89 = bf16[768,3072]{1,0:T(8,128)(2,1)} copy(bf16[768,3072]{0,1:T(8,128)(2,1)} %fusion.10) | data formatting | bytes 9437184 | tf_op jit(solution)/shard_map/convert_element_type | solution.py:828
  377.0 9.8 %reshape.269 = bf16[8,96,4,768]{3,2,1,0:T(4,128)(2,1)} reshape(bf16[768,3072]{1,0:T(8,128)(2,1)} %copy.89) | data formatting | bytes 9437184 | tf_op jit(solution)/shard_map/reshape | solution.py:829
  386.7 9.7 %reshape.268 = bf16[8,96,4,768]{3,2,1,0:T(4,128)(2,1)} reshape(bf16[768,3072]{1,0:T(8,128)(2,1)} %convolution_convert_fusion.1) | data formatting | bytes 9437184 | tf_op jit(solution)/shard_map/reshape | solution.py:829
  396.4 9.3 %pad_maximum_fusion = bf16[8,4,96,1728]{3,1,2,0:T(4,128)(2,1)S(1)} fusion(bf16[8,4,96,192]{3,1,2,0:T(4,128)(2,1)} %bitcast.157, bf16[8,4,96,768]{3,1,2,0:T(4,128)(2,1)} %bitcast.146, bf16[8,4,96,768]{3,1,2,0:T(4,128)(2,1)} %bitcast.147), kind=kLoop, calls=%fused_computation | loop fusion | flops 31850496 | bytes 21233664 | tf_op jit(solution)/shard_map/concatenate | solution.py:833
  405.8 5.2 copy.90
  411.1 19.9 %attn_dq.1 = bf16[2048,192]{1,0:T(8,128)(2,1)} custom-call(s32[17]{0:T(128)} %pad_add_fusion.meta, bf16[2048,256]{1,0:T(8,128)(2,1)} %get-tuple-element.35.q_ref, bf16[2048,256]{1,0:T(8,128)(2,1)} %pad_maximum_fusion.4.do_ref, bf16[6144,256]{1,0:T(8,128)(2,1)} %get-tuple-element.121.k_ref, bf16[6144,256]{1,0:T(8,128)(2,1)} %get-tuple-element.120.v_ref), custom_call_target="tpu_custom_call" | custom-call | flops 44999999488 | bytes 12582912 | tf_op jit(solution)/shard_map/attn_dq/pallas_call | solution.py:638
  431.0 2.8 convolution_convert_fusion.9
  435.1 4.8 fusion.39
  439.9 9.4 %add_convert_fusion = bf16[512,768]{1,0:T(8,128)(2,1)} fusion(f32[512,768]{1,0:T(8,128)S(1)} %copy-done.14, bf16[768,3072]{1,0:T(8,128)(2,1)} %bitcast.159, f32[512,3072]{1,0:T(8,128)} %copy-done.56), kind=kOutput, calls=%fused_computation.55 | convolution fusion | flops 2430861312 | bytes 13369344 | tf_op jit(solution)/shard_map/dot_general | solution.py:30
  449.4 6.0 pad_maximum_fusion.2.do_ref
  455.4 51.0 %attn_dkv.1 = (bf16[2048,192]{1,0:T(8,128)(2,1)}, bf16[2048,192]{1,0:T(8,128)(2,1)}) custom-call(s32[17]{0:T(128)} %pad_add_fusion.meta, bf16[2048,256]{1,0:T(8,128)(2,1)} %slice.121.k_ref, bf16[2048,256]{1,0:T(8,128)(2,1)} %slice.122.v_ref, bf16[6144,256]{1,0:T(8,128)(2,1)} %pad_maximum_fusion.1.q_ref, bf16[6144,256]{1,0:T(8,128)(2,1)} %pad_maximum_fusion.2.do_ref), custom_call_target="tpu_custom_call" | custom-call | flops 60000002048 | bytes 12582912 | tf_op jit(solution)/shard_map/attn_dkv/pallas_call | solution.py:694
  506.4 2.2 convolution_convert_fusion.8
  508.8 2.8 convolution_convert_fusion.7
  514.7 5.1 multiply_reduce_fusion
  520.0 85.3 %tail.1 = (f32[512,768]{1,0:T(8,128)S(1)}, f32[96,192]{1,0:T(8,128)S(1)}, f32[96,192]{1,0:T(8,128)S(1)}, f32[96,96]{1,0:T(8,128)S(1)}, bf16[2,512,192]{2,1,0:T(8,128)(2,1)S(1)}, /*index=5*/f32[2,1,96]{2,1,0:T(1,128)S(1)}) custom-call(bf16[4,512,768]{2,1,0:T(8,128)(2,1)} %bitcast.150, bf16[8,96,192]{2,1,0:T(8,128)(2,1)S(1)} %bitcast.139, ...), custom_call_target="tpu_custom_call" | custom-call | tf_op jit(solution)/shard_map/tail/pallas_call | solution.py:453
  607.5 1.7 fusion.19
  (212 shorter events, 51.8 us)
Async XLA Ops:
  7.2 267.3 %all-gather.3.cloned.1.call-start = ((), (), s32[]{:S(2)}) async-start(), calls=%async_computation.2 | async-start | bytes 11354112 | tf_op jit(solution)/shard_map/all_gather | solution.py:757
  9.9 599.4 %reduce-scatter.2.cloned.1.call-start = ((), (), s32[]{:S(2)}) async-start(), calls=%async_computation.1 | async-start | bytes 11354112 | tf_op jit(solution)/shard_map/reduce_scatter | solution.py:835
  66.9 3.4 copy-start.1
  67.8 10.7 %copy-start.45 = (f32[768]{0:T(1024)}, f32[768]{0:T(1024)S(1)}, u32[]{:S(2)}) copy-start(f32[768]{0:T(1024)S(1)} %mul.176) | copy-start | bytes 9220
  67.8 5.4 copy-start.42
  75.2 3.3 copy-start.51
  81.8 4.9 copy-start.20
  81.8 6.4 %copy-start.22 = (bf16[2048,128]{1,0:T(8,128)(2,1)}, bf16[2048,128]{1,0:T(8,128)(2,1)S(1)}, u32[]{:S(2)}) copy-start(bf16[2048,128]{1,0:T(8,128)(2,1)S(1)} %slice.110) | copy-start | bytes 1572868
  81.8 4.8 copy-start.16
  81.8 4.8 copy-start.18
  88.2 55.9 %copy-start.55 = (s32[16]{0:T(128)S(1)}, s32[16]{0:T(128)}, u32[]{:S(2)}) copy-start(s32[16]{0:T(128)} %param.23) | copy-start | bytes 196
  143.8 4.6 copy-start.8
  202.6 68.8 %collective-permute-start.1 = (bf16[2048,256]{1,0:T(8,128)(2,1)}, bf16[2048,256]{1,0:T(8,128)(2,1)}, u32[]{:S(2)}, u32[]{:S(2)}) collective-permute-start(bf16[2048,256]{1,0:T(8,128)(2,1)} %get-tuple-element.35.q_ref), channel_id=1, source_target_pairs={{2,0},{3,1},{4,2},{5,3},{6,4},{7,5},{10,8},{11,9},{12,10},{13,11},... | collective-permute-start | bytes 3145736 | tf_op jit(solution)/shard_map/ppermute | solution.py:845
  203.9 67.5 %collective-permute-start = (bf16[2048,256]{1,0:T(8,128)(2,1)}, bf16[2048,256]{1,0:T(8,128)(2,1)}, u32[]{:S(2)}, u32[]{:S(2)}) collective-permute-start(bf16[2048,256]{1,0:T(8,128)(2,1)} %get-tuple-element.35.q_ref), channel_id=1, source_target_pairs={{1,0},{2,1},{3,2},{4,3},{5,4},{6,5},{7,6},{9,8},{10,9},{11,10},{12... | collective-permute-start | bytes 3145736 | tf_op jit(solution)/shard_map/ppermute | solution.py:845
  207.6 18.1 %copy-start.3 = (bf16[512,768]{1,0:T(8,128)(2,1)S(1)}, bf16[512,768]{1,0:T(8,128)(2,1)}, u32[]{:S(2)}) copy-start(bf16[512,768]{1,0:T(8,128)(2,1)} %tok.1) | copy-start | bytes 2359300
  209.9 61.5 %copy-start.35 = (bf16[2048,256]{1,0:T(8,128)(2,1)S(1)}, bf16[2048,256]{1,0:T(8,128)(2,1)}, u32[]{:S(2)}) copy-start(bf16[2048,256]{1,0:T(8,128)(2,1)} %get-tuple-element.35.q_ref) | copy-start | bytes 3145732
  225.5 78.1 %copy-start.25 = (bf16[512,4,192]{0,2,1:T(8,128)(2,1)}, bf16[512,4,192]{0,2,1:T(8,128)(2,1)S(1)}, u32[]{:S(2)}) copy-start(bf16[512,4,192]{0,2,1:T(8,128)(2,1)S(1)} %copy.75) | copy-start | bytes 2359300
  225.8 48.7 %copy-start.49 = (f32[512]{0:T(512)}, f32[512]{0:T(512)S(1)}, u32[]{:S(2)}) copy-start(f32[512]{0:T(512)S(1)} %broadcast_multiply_fusion.3) | copy-start | bytes 6148
  289.4 14.2 %copy-start.32 = (bf16[768,768]{0,1:T(8,128)(2,1)}, bf16[768,768]{0,1:T(8,128)(2,1)S(1)}, u32[]{:S(2)}) copy-start(bf16[768,768]{0,1:T(8,128)(2,1)S(1)} %reshape.256) | copy-start | bytes 3538948
  295.8 2.6 slice-start
  295.8 3.1 slice-start.1
  296.9 10.9 %copy-start.24 = (bf16[96,8,4,768]{3,1,2,0:T(8,128)(2,1)}, bf16[96,8,4,768]{3,1,2,0:T(8,128)(2,1)S(1)}, u32[]{:S(2)}) copy-start(bf16[96,8,4,768]{3,1,2,0:T(8,128)(2,1)S(1)} %copy.101) | copy-start | bytes 14155780
  304.5 14.1 %copy-start.13 = (f32[512,768]{1,0:T(8,128)}, f32[512,768]{1,0:T(8,128)S(1)}, u32[]{:S(2)}) copy-start(f32[512,768]{1,0:T(8,128)S(1)} %get-tuple-element.123) | copy-start | bytes 4718596
  304.9 3.0 copy-start.36
  307.8 7.3 %copy-start.56 = (f32[512,3072]{1,0:T(8,128)}, f32[512,3072]{1,0:T(8,128)S(1)}, u32[]{:S(2)}) copy-start(f32[512,3072]{1,0:T(8,128)S(1)} %fusion.33) | copy-start | bytes 18874372
  315.1 3.5 copy-start.57
  319.9 30.9 %copy-start.6 = (f32[512,768]{1,0:T(8,128)}, f32[512,768]{1,0:T(8,128)S(1)}, u32[]{:S(2)}) copy-start(f32[512,768]{1,0:T(8,128)S(1)} %multiply_add_fusion.2) | copy-start | bytes 4718596
  339.9 5.6 copy-start.5
  339.9 5.6 copy-start.11
  345.5 5.3 copy-start.26
  345.5 7.1 %copy-start.37 = (bf16[512,768]{1,0:T(8,128)(2,1)S(1)}, bf16[512,768]{1,0:T(8,128)(2,1)}, u32[]{:S(2)}) copy-start(bf16[512,768]{1,0:T(8,128)(2,1)} %param.14) | copy-start | bytes 2359300
  348.2 101.1 %collective-permute-start.3 = (bf16[2048,256]{1,0:T(8,128)(2,1)}, bf16[2048,256]{1,0:T(8,128)(2,1)}, u32[]{:S(2)}, u32[]{:S(2)}) collective-permute-start(bf16[2048,256]{1,0:T(8,128)(2,1)} %pad_maximum_fusion.4.do_ref), channel_id=1, source_target_pairs={{2,0},{3,1},{4,2},{5,3},{6,4},{7,5},{10,8},{11,9},{12,10},{13,11},... | collective-permute-start | bytes 3145736 | tf_op jit(solution)/shard_map/ppermute | solution.py:845
  349.5 99.9 %collective-permute-start.2 = (bf16[2048,256]{1,0:T(8,128)(2,1)}, bf16[2048,256]{1,0:T(8,128)(2,1)}, u32[]{:S(2)}, u32[]{:S(2)}) collective-permute-start(bf16[2048,256]{1,0:T(8,128)(2,1)} %pad_maximum_fusion.4.do_ref), channel_id=1, source_target_pairs={{1,0},{2,1},{3,2},{4,3},{5,4},{6,5},{7,6},{9,8},{10,9},{11,10},{12... | collective-permute-start | bytes 3145736 | tf_op jit(solution)/shard_map/ppermute | solution.py:845
  352.7 8.4 %copy-start.14 = (f32[512,768]{1,0:T(8,128)S(1)}, f32[512,768]{1,0:T(8,128)}, u32[]{:S(2)}) copy-start(f32[512,768]{1,0:T(8,128)} %copy-done.13) | copy-start | bytes 4718596
  352.7 8.4 %copy-start.58 = (bf16[512,3072]{1,0:T(8,128)(2,1)S(1)}, bf16[512,3072]{1,0:T(8,128)(2,1)}, u32[]{:S(2)}) copy-start(bf16[512,3072]{1,0:T(8,128)(2,1)} %copy-done.57) | copy-start | bytes 9437188
  411.1 20.0 %copy-start.28 = (bf16[2048,768]{1,0:T(8,128)(2,1)S(1)}, bf16[2048,768]{1,0:T(8,128)(2,1)}, u32[]{:S(2)}) copy-start(bf16[2048,768]{1,0:T(8,128)(2,1)} %copy-done.27) | copy-start | bytes 9437188
  431.0 4.0 copy-start.53
  431.0 4.0 copy-start.31
  439.9 9.4 %copy-start.12 = (bf16[2048,55]{1,0:T(8,128)(2,1)S(1)}, bf16[2048,55]{1,0:T(8,128)(2,1)}, u32[]{:S(2)}) copy-start(bf16[2048,55]{1,0:T(8,128)(2,1)} %copy-done.10) | copy-start | bytes 675844
  439.9 9.4 %copy-start.15 = (bf16[2048,9]{1,0:T(8,128)(2,1)S(1)}, bf16[2048,9]{1,0:T(8,128)(2,1)}, u32[]{:S(2)}) copy-start(bf16[2048,9]{1,0:T(8,128)(2,1)} %copy.85) | copy-start | bytes 110596
  455.4 51.0 %copy-start.29 = (bf16[2048,768]{1,0:T(8,128)(2,1)S(1)}, bf16[2048,768]{1,0:T(8,128)(2,1)}, u32[]{:S(2)}) copy-start(bf16[2048,768]{1,0:T(8,128)(2,1)} %copy-done.27) | copy-start | bytes 9437188
  506.4 2.4 copy-start
  508.8 3.6 copy-start.39
  508.8 3.6 copy-start.41
  519.9 87.0 %copy-start.4 = (bf16[512,768]{1,0:T(8,128)(2,1)S(1)}, bf16[512,768]{1,0:T(8,128)(2,1)}, u32[]{:S(2)}) copy-start(bf16[512,768]{1,0:T(8,128)(2,1)} %tok.1) | copy-start | bytes 2359300
  520.0 86.9 %copy-start.46 = (f32[768]{0:T(1024)S(1)}, f32[768]{0:T(1024)}, u32[]{:S(2)}) copy-start(f32[768]{0:T(1024)} %copy-done.45) | copy-start | bytes 9220
  520.0 86.9 %copy-start.50 = (f32[512]{0:T(512)S(1)}, f32[512]{0:T(512)}, u32[]{:S(2)}) copy-start(f32[512]{0:T(512)} %copy-done.49) | copy-start | bytes 6148
  520.0 86.9 %copy-start.52 = (f32[512]{0:T(512)S(1)}, f32[512]{0:T(512)}, u32[]{:S(2)}) copy-start(f32[512]{0:T(512)} %add_rsqrt_fusion.1) | copy-start | bytes 6148
  (19 other events, 33.3 us)
Sparse Core Ops, SparseCore 0:
  10.9 116.5 all-gather.2
  411.2 180.2 reduce-scatter.1

commit v2 on v1

v2 whole, which is shorter than its diff:
```python
import functools

import jax
import jax.numpy as jnp
from jax import lax
from jax.experimental import pallas as pl
from jax.experimental.pallas import tpu as pltpu
from jax.sharding import PartitionSpec as P

HEADS = 12
HEAD_DIM = 64
DOC_MAX = 4096
EPSILON = 1e-05
GELU_SCALE = 0.7978845608028654
EXCLUDED = -1e30
WIDTH = 256
SPLITS = 3
BF16 = jnp.bfloat16
F32 = jnp.float32
MESH = pl.DeviceIdType.MESH
ANY = pl.BlockSpec(memory_space=pl.ANY)
WHOLE = pl.BlockSpec(memory_space=pltpu.VMEM)
NT = (((1,), (1,)), ((), ()))
TN = (((0,), (0,)), ((), ()))


def dotf(left, right, dims=None):
    if dims is None:
        dims = (((1,), (0,)), ((), ()))
    return lax.dot_general(left, right, dims, preferred_element_type=F32)


def remote(src, dst, send_sem, recv_sem, head, blk):
    return pltpu.make_async_remote_copy(
        src_ref=src,
        dst_ref=dst,
        send_sem=send_sem,
        recv_sem=recv_sem,
        device_id={"head": head, "blk": blk},
        device_id_type=MESH,
    )


def greet(partners):
    barrier = pltpu.get_barrier_semaphore()
    for head, blk in partners:
        pl.semaphore_signal(
            barrier, inc=1, device_id={"head": head, "blk": blk}, device_id_type=MESH
        )
    pl.semaphore_wait(barrier, len(partners))


def xor(value, bit):
    return value + bit - 2 * bit * (lax.div(value, bit) % 2)


def partners_of(head, blk, nblk, heads=True, blks=True):
    found = []
    if heads:
        found += [(xor(head, 1), blk), (xor(head, 2), blk), (3 - head, blk)]
    if blks:
        found += [(head, lax.rem(blk + d, nblk)) for d in range(1, nblk)]
    return found


class Line:
    def __init__(self, nblk, head, blk, sources, targets, up, down, across):
        self.half, self.head, self.blk = nblk // 2, head, blk
        self.place, self.parity = lax.div(blk, 2), lax.rem(blk, 2)
        self.sources, self.targets = sources, targets
        self.sems = {"up": up, "down": down, "across": across}

    def copies(self, way, origin, step, fresh=False):
        slot = 2 * origin + self.parity
        to = {
            "up": lax.rem(self.blk + 2, 2 * self.half),
            "down": lax.rem(self.blk + 2 * self.half - 2, 2 * self.half),
            "across": self.blk + 1 - 2 * self.parity,
        }[way]
        send, recv = self.sems[way]
        return [
            remote(
                source if fresh else target.at[slot],
                target.at[slot],
                send.at[k, step],
                recv.at[k, step],
                self.head,
                to,
            )
            for k, (source, target) in enumerate(zip(self.sources, self.targets))
        ]

    def landing(self, way, origin, step, parity=None):
        slot = 2 * origin + (self.parity if parity is None else parity)
        send, recv = self.sems[way]
        other = self.blk + 1 - 2 * self.parity
        return [
            remote(
                target.at[slot], target.at[slot], send.at[k, step], recv.at[k, step], self.head, other
            )
            for k, target in enumerate(self.targets)
        ]

    def each(self, condition, copies, verb):
        @pl.when(condition)
        def _():
            for copy in copies():
                getattr(copy, verb)()

    def begin(self):
        self.each(self.place + 1 < self.half, lambda: self.copies("up", self.place, 0, True), "start")
        self.each(self.place > 0, lambda: self.copies("down", self.place, 0, True), "start")
        for copy in self.copies("across", self.place, self.place, True):
            copy.start()

    def step(self, s):
        low, high = self.place - 1 - s, self.place + 1 + s
        self.each(low >= 0, lambda: self.landing("up", low, s), "wait_recv")
        if s + 1 < self.half - 1:
            self.each(
                (low >= 0) & (self.place + 1 < self.half),
                lambda: self.copies("up", low, s + 1),
                "start",
            )
        self.each(low >= 0, lambda: self.copies("across", low, low), "start")
        self.each(high < self.half, lambda: self.landing("down", high, s), "wait_recv")
        if s + 1 < self.half - 1:
            self.each(
                (high < self.half) & (self.place > 0),
                lambda: self.copies("down", high, s + 1),
                "start",
            )
        self.each(high < self.half, lambda: self.copies("across", high, high), "start")

    def end(self):
        for o in range(self.half):
            for copy in self.landing("across", o, o, 1 - self.parity):
                copy.wait_recv()
            for copy in self.copies("across", o, o):
                copy.wait_send()
        for s in range(self.half - 1):
            self.each(
                (self.place - s >= 0) & (self.place + 1 < self.half),
                lambda: self.copies("up", self.place - s, s),
                "wait_send",
            )
            self.each(
                (self.place + s < self.half) & (self.place > 0),
                lambda: self.copies("down", self.place + s, s),
                "wait_send",
            )


def front_kernel(
    nblk, pieces, tok, first, w_qk, w_rest, w_v, gains,
    tok_all, first_all, qk_all, rest_all, v_own, v_all, gain_all,
    own_sem, send_x, recv_x, send_s, recv_s, send_f, recv_f, send_w, recv_w, send_v, recv_v,
    send_u, recv_u, send_d, recv_d, send_y, recv_y,
):
    head, blk = lax.axis_index("head"), lax.axis_index("blk")
    side, core, far = xor(head, 2), xor(head, 1), 3 - head
    greet(partners_of(head, blk, nblk))
    moved = [(tok, tok_all), (first, first_all)]
    weights = [(w_v, v_own), (gains, gain_all)]
    large = [(w_qk, qk_all), (w_rest, rest_all)]
    rows = tok.shape[0] // pieces
    line = Line(
        nblk, head, blk, [w_qk, w_rest], [qk_all, rest_all],
        (send_u, recv_u), (send_d, recv_d), (send_y, recv_y),
    )

    def part(ref, p):
        return ref.at[pl.ds(p * rows, rows)]

    def hop(sems, k, p, source, slot, target):
        dst = part(moved[k][1].at[slot], p)
        return remote(source, dst, sems[0].at[k, p], sems[1].at[k, p], target, blk)

    xs, ss, fs = (send_x, recv_x), (send_s, recv_s), (send_f, recv_f)
    order = [(k, p) for p in range(pieces) for k in range(2)]
    line.begin()
    for k, p in order:
        hop(xs, k, p, part(moved[k][0], p), head, side).start()

    def spread(d):
        to = lax.rem(blk + d, nblk)
        return [
            remote(src, dst.at[blk], send_w.at[i, d], recv_w.at[i, d], head, to)
            for i, (src, dst) in enumerate(weights)
        ]

    def from_peer(d):
        source = lax.rem(blk - d + nblk, nblk)
        return [
            remote(src, dst.at[source], send_w.at[i, d], recv_w.at[i, d], head, source)
            for i, (src, dst) in enumerate(weights)
        ]

    for d in range(1, nblk):
        for copy in spread(d):
            copy.start()
    for k, p in order:
        hop(ss, k, p, part(moved[k][0], p), head, core).start()
    local = [
        pltpu.make_async_copy(moved[k][0], moved[k][1].at[head], own_sem.at[k]) for k in range(2)
    ] + [
        pltpu.make_async_copy(src, dst.at[blk], own_sem.at[2 + i])
        for i, (src, dst) in enumerate(weights + large)
    ]
    for copy in local:
        copy.start()

    def pass_on(k, p):
        landed = part(moved[k][1].at[side], p)
        hop(xs, k, p, landed, side, side).wait_recv()
        hop(fs, k, p, landed, side, core).start()

    steps = nblk // 2 - 1
    for s in range(steps):
        line.step(s)
        for k, p in order[s * len(order) // steps : (s + 1) * len(order) // steps]:
            pass_on(k, p)
    for copy in local:
        copy.wait()
    for d in range(1, nblk):
        for copy in from_peer(d):
            copy.wait_recv()
    half, kind = lax.div(head, 2), lax.rem(head, 2)
    for i in range(2):
        target = half + 2 * i

        @pl.when(target == head)
        def _():
            pltpu.make_async_copy(v_own, v_all.at[kind], own_sem.at[6]).start()

        @pl.when(target != head)
        def _():
            remote(v_own, v_all.at[kind], send_v.at[i], recv_v.at[kind], target, blk).start()

    for k, p in order:
        hop(ss, k, p, part(moved[k][1].at[core], p), core, core).wait_recv()
        hop(fs, k, p, part(moved[k][1].at[far], p), far, core).wait_recv()
    for c in range(2):
        source = 2 * kind + c

        @pl.when(source == head)
        def _():
            pltpu.make_async_copy(v_own, v_all.at[c], own_sem.at[6]).wait()

        @pl.when(source != head)
        def _():
            remote(v_own, v_all.at[c], send_v.at[0], recv_v.at[c], source, blk).wait_recv()

    for i in range(2):
        target = half + 2 * i

        @pl.when(target != head)
        def _():
            remote(v_own, v_all.at[kind], send_v.at[i], recv_v.at[kind], target, blk).wait_send()

    for k, p in order:
        hop(xs, k, p, part(moved[k][0], p), head, side).wait_send()
        hop(ss, k, p, part(moved[k][0], p), head, core).wait_send()
        hop(fs, k, p, part(moved[k][1].at[side], p), side, core).wait_send()
    for d in range(1, nblk):
        for copy in spread(d):
            copy.wait_send()
    line.end()


def front(nblk, tok, first, w_qk, w_rest, w_v, gains, pieces=4):
    def shape(lead, like):
        return jax.ShapeDtypeStruct(lead + like.shape, like.dtype)

    dma = pltpu.SemaphoreType.DMA
    return pl.pallas_call(
        functools.partial(front_kernel, nblk, pieces),
        out_shape=[
            shape((4,), tok),
            shape((4,), first),
            shape((nblk,), w_qk),
            shape((nblk,), w_rest),
            shape((nblk,), w_v),
            shape((2, nblk), w_v),
            shape((nblk,), gains),
        ],
        in_specs=[WHOLE] * 6,
        out_specs=[ANY] * 7,
        scratch_shapes=[dma((7,))]
        + [dma((2, pieces))] * 6
        + [dma((2, nblk))] * 2
        + [dma((2,))] * 2
        + [dma((2, nblk // 2))] * 6,
        compiler_params=pltpu.CompilerParams(collective_id=0, has_side_effects=True),
        name="front",
    )(tok, first, w_qk, w_rest, w_v, gains)


def halo_kernel(
    nblk, pieces, own, rest, near_far, rest_all,
    send_z, recv_z, send_y, recv_y, send_x, recv_x, send_c, recv_c, send_f, recv_f,
):
    head, blk = lax.axis_index("head"), lax.axis_index("blk")
    side, core, beyond = xor(head, 2), xor(head, 1), 3 - head
    odd = lax.rem(blk, 2)
    pair = blk + 1 - 2 * odd
    up, down = lax.rem(blk + 2, nblk), lax.rem(blk + nblk - 2, nblk)
    greet(partners_of(head, blk, nblk, blks=False) + [(head, pair), (head, up), (head, down)])
    rows = own.shape[0] // pieces

    def part(ref, p):
        return ref.at[pl.ds(p * rows, rows)]

    def far_copy(p, to):
        return remote(part(own, p), part(near_far.at[0], p), send_z.at[p], recv_z.at[p], head, to)

    def near_copy(p, src):
        return remote(src, part(near_far.at[1], p), send_y.at[p], recv_y.at[p], head, pair)

    def chunk(sems, b, source, slot, to):
        return remote(
            source, rest_all.at[slot, b], sems[0].at[b], sems[1].at[b], to, blk
        )

    xs, cs, fs = (send_x, recv_x), (send_c, recv_c), (send_f, recv_f)
    for p in range(pieces):

        @pl.when(blk + 2 < nblk)
        def _():
            far_copy(p, up).start()

        @pl.when(odd == 0)
        def _():
            near_copy(p, part(own, p)).start()

    for b in range(nblk):
        chunk(xs, b, rest.at[b], head, side).start()
    for b in range(nblk):
        chunk(cs, b, rest.at[b], head, core).start()
    for n in range(max(pieces, nblk)):
        if n < pieces:

            @pl.when(blk >= 2)
            def _():
                far_copy(n, down).wait_recv()

            @pl.when((blk >= 2) & (odd == 1))
            def _():
                near_copy(n, part(near_far.at[0], n)).start()

        if n < nblk:
            landed = rest_all.at[side, n]
            chunk(xs, n, landed, side, side).wait_recv()
            chunk(fs, n, landed, side, core).start()
    for b in range(nblk):
        chunk(cs, b, rest.at[b], core, core).wait_recv()
        chunk(fs, b, rest.at[b], beyond, core).wait_recv()
    for b in range(nblk):
        chunk(xs, b, rest.at[b], head, side).wait_send()
        chunk(cs, b, rest.at[b], head, core).wait_send()
        chunk(fs, b, rest_all.at[side, b], side, core).wait_send()
    for p in range(pieces):

        @pl.when((blk >= 2) | (odd == 1))
        def _():
            near_copy(p, part(own, p)).wait_recv()

        @pl.when(blk + 2 < nblk)
        def _():
            far_copy(p, up).wait_send()

        @pl.when((blk >= 2) | (odd == 0))
        def _():
            near_copy(p, part(own, p)).wait_send()


def halo(nblk, own, rest, pieces=8):
    dma = pltpu.SemaphoreType.DMA
    return pl.pallas_call(
        functools.partial(halo_kernel, nblk, pieces),
        out_shape=[
            jax.ShapeDtypeStruct((2,) + own.shape, own.dtype),
            jax.ShapeDtypeStruct((4,) + rest.shape, rest.dtype),
        ],
        in_specs=[ANY] * 2,
        out_specs=[ANY] * 2,
        scratch_shapes=[dma((pieces,))] * 4 + [dma((nblk,))] * 6,
        compiler_params=pltpu.CompilerParams(collective_id=1, has_side_effects=True),
        name="halo",
    )(own, rest)


def tail_kernel(
    nblk, pieces, cols, grad, weights, first, gains, kept, got,
    out_grad, out_qk, out_v, out_first, out_gain, out_rest,
    core_buf, side_out, side_buf, pair_buf, line_out, line_in, v_sum, v_got,
    gain_buf, gain_sum, gain_got, up_out, up_in, down_out, down_in,
    own_sem, send_s, recv_s, send_x, recv_x, send_y, recv_y, send_l, recv_l,
    send_v, recv_v, send_f, recv_f, send_g, recv_g, send_h, recv_h, send_u, recv_u, send_d, recv_d,
):
    head, blk = lax.axis_index("head"), lax.axis_index("blk")
    side, core, far = xor(head, 2), xor(head, 1), 3 - head
    greet(partners_of(head, blk, nblk))
    rows = grad.shape[1] // pieces
    line, place, parity = nblk // 2, lax.div(blk, 2), lax.rem(blk, 2)
    pair = blk + 1 - 2 * parity
    above, below = lax.rem(blk + 2, nblk), lax.rem(blk + nblk - 2, nblk)

    def part(ref, p):
        return ref.at[pl.ds(p * rows, rows)]

    def to_core(i, p, slot):
        return remote(
            part(grad.at[slot], p), part(core_buf.at[i], p), send_s.at[i, p], recv_s.at[i, p],
            core, blk,
        )

    def to_side(p):
        return remote(
            part(side_out, p), part(side_buf, p), send_x.at[p], recv_x.at[p], side, blk
        )

    def sum_of(t):
        return kept[t].astype(F32) + got[t].astype(F32)

    def up_copy(t, to):
        return remote(up_out.at[t], up_in.at[t], send_u.at[t], recv_u.at[t], head, to)

    def down_copy(t, to):
        return remote(down_out.at[t], down_in.at[t], send_d.at[t], recv_d.at[t], head, to)

    def first_hops():
        for n in range(line - 1):
            t = line - 1 - n

            @pl.when((place == 0) & (place < t))
            def _():
                up_out[t] = sum_of(t).astype(BF16)
                up_copy(t, above).start()

            @pl.when((place == line - 1) & (place > n))
            def _():
                down_out[n] = sum_of(n).astype(BF16)
                down_copy(n, below).start()

    def next_hops(n):
        t = line - 1 - n

        @pl.when((place > 0) & (place < t))
        def _():
            up_copy(t, above).wait_recv()
            up_out[t] = (sum_of(t) + up_in[t].astype(F32)).astype(BF16)
            up_copy(t, above).start()

        @pl.when((place < line - 1) & (place > n))
        def _():
            down_copy(n, below).wait_recv()
            down_out[n] = (sum_of(n) + down_in[n].astype(F32)).astype(BF16)
            down_copy(n, below).start()

    for p in range(pieces):
        to_core(0, p, far).start()
    first_hops()
    for p in range(pieces):
        to_core(1, p, core).start()

    def across(n):
        return remote(
            weights.at[2 * n + 1 - parity], pair_buf.at[n], send_y.at[n], recv_y.at[n], head, pair
        )

    for n in range(line):
        across(n).start()
    half, kind = lax.div(head, 2), lax.rem(head, 2)

    def gain_to(d):
        to = lax.rem(blk + d, nblk)
        return remote(gains.at[to], gain_buf.at[blk], send_g.at[d], recv_g.at[d], head, to)

    def gain_from(d):
        source = lax.rem(blk - d + nblk, nblk)
        return remote(gains.at[0], gain_buf.at[source], send_g.at[d], recv_g.at[d], head, source)

    for d in range(1, nblk):
        gain_to(d).start()
    gain_buf[blk] = gains[blk]

    def first_copy(i, to, slot):
        return remote(first.at[to], out_first.at[slot], send_f.at[i], recv_f.at[slot], to, blk)

    @pl.when(half == 1)
    def _():
        for i, to in enumerate((core, side, far)):
            first_copy(i, to, kind).start()
        pltpu.make_async_copy(first.at[head], out_first.at[kind], own_sem).start()

    for p in range(pieces):
        to_core(0, p, far).wait_recv()
        part(side_out, p)[...] = (
            part(grad.at[side], p)[...].astype(F32) + part(core_buf.at[0], p)[...].astype(F32)
        ).astype(BF16)
        to_side(p).start()

    def along(d, to):
        return remote(
            line_out.at[to], line_in.at[d], send_l.at[d], recv_l.at[d], head, 2 * to + parity
        )

    for n in range(line):
        across(n).wait_recv()
        line_out[n] = (
            weights[2 * n + parity].astype(F32) + pair_buf[n].astype(F32)
        ).astype(BF16)
    for d in range(1, line):
        along(d, lax.rem(place + d, line)).start()
    for d in range(1, nblk):
        gain_from(d).wait_recv()
    gain_sum[...] = jnp.sum(gain_buf[...], axis=0)
    peers = (core, side, far)

    def gain_copy(i, to):
        return remote(gain_sum, gain_got.at[i], send_h.at[i], recv_h.at[i], to, blk)

    for i, to in enumerate(peers):
        gain_copy(i, to).start()
    for n in range(line - 1):
        next_hops(n)
    total = line_out[place].astype(F32)
    for d in range(1, line):
        along(d, lax.rem(place - d + line, line)).wait_recv()
        total = total + line_in[d].astype(F32)
    out_qk[...] = total[:, : 2 * cols]
    v_sum[0] = total[:, 2 * cols : 2 * cols + cols // 2]
    v_sum[1] = total[:, 2 * cols + cols // 2 : 3 * cols]

    def give(c, to):
        return remote(v_sum.at[c], v_got, send_v.at[c], recv_v.at[0], to, blk)

    for c in range(2):
        to = 2 * head + c

        @pl.when((half == 0) & (to != head))
        def _():
            give(c, to).start()

    for p in range(pieces):
        to_core(1, p, core).wait_recv()
        to_side(p).wait_recv()
        part(out_grad, p)[...] = (
            part(grad.at[head], p)[...].astype(F32)
            + part(core_buf.at[1], p)[...].astype(F32)
            + part(side_buf, p)[...].astype(F32)
        )
    out_rest[...] = sum_of(place)
    for t in range(line):

        @pl.when((place == t) & (place > 0))
        def _():
            up_copy(t, above).wait_recv()
            out_rest[...] += up_in[t].astype(F32)

        @pl.when((place == t) & (place < line - 1))
        def _():
            down_copy(t, below).wait_recv()
            out_rest[...] += down_in[t].astype(F32)

    for i, to in enumerate(peers):
        gain_copy(i, to).wait_recv()
    out_gain[...] = gain_sum[...] + gain_got[0] + gain_got[1] + gain_got[2]

    @pl.when(head == 0)
    def _():
        out_v[...] = v_sum[0]

    @pl.when(head != 0)
    def _():
        give(0, half).wait_recv()
        out_v[...] = v_got[...]

    for slot in range(2):

        @pl.when(head == 2 + slot)
        def _():
            pltpu.make_async_copy(first.at[head], out_first.at[slot], own_sem).wait()

        @pl.when(head != 2 + slot)
        def _():
            first_copy(0, 2 + slot, slot).wait_recv()

    @pl.when(half == 1)
    def _():
        for i, to in enumerate((core, side, far)):
            first_copy(i, to, kind).wait_send()

    for c in range(2):
        to = 2 * head + c

        @pl.when((half == 0) & (to != head))
        def _():
            give(c, to).wait_send()

    for i, to in enumerate(peers):
        gain_copy(i, to).wait_send()
    for p in range(pieces):
        to_core(0, p, far).wait_send()
        to_core(1, p, core).wait_send()
        to_side(p).wait_send()
    for d in range(1, nblk):
        gain_to(d).wait_send()
    for n in range(line):
        across(n).wait_send()
    for d in range(1, line):
        along(d, lax.rem(place + d, line)).wait_send()
    for t in range(line):

        @pl.when(place < t)
        def _():
            up_copy(t, above).wait_send()

        @pl.when(place > t)
        def _():
            down_copy(t, below).wait_send()


def tail(nblk, grad, weights, first, gains, kept, got, cols, pieces=4):
    dma = pltpu.SemaphoreType.DMA
    row, part = grad.shape[1:], weights.shape[1]
    half, line = (part, cols // 2), nblk // 2
    piece = (2, pieces)
    vmem = lambda *shape: pltpu.VMEM(shape, BF16)
    return pl.pallas_call(
        functools.partial(tail_kernel, nblk, pieces, cols),
        out_shape=[
            jax.ShapeDtypeStruct(row, F32),
            jax.ShapeDtypeStruct((part, 2 * cols), F32),
            jax.ShapeDtypeStruct(half, F32),
            jax.ShapeDtypeStruct((2,) + first.shape[1:], BF16),
            jax.ShapeDtypeStruct(gains.shape[1:], F32),
            jax.ShapeDtypeStruct(kept.shape[1:], F32),
        ],
        in_specs=[WHOLE] * 6,
        out_specs=[WHOLE] * 6,
        scratch_shapes=[
            vmem(2, *row), vmem(*row), vmem(*row),
            vmem(line, *weights.shape[1:]), vmem(line, *weights.shape[1:]),
            vmem(line, *weights.shape[1:]),
            pltpu.VMEM((2,) + half, F32),
            pltpu.VMEM(half, F32),
            pltpu.VMEM(gains.shape, F32),
            pltpu.VMEM(gains.shape[1:], F32),
            pltpu.VMEM((3,) + gains.shape[1:], F32),
            vmem(*kept.shape), vmem(*kept.shape), vmem(*kept.shape), vmem(*kept.shape),
            dma,
            dma(piece), dma(piece),
            dma((pieces,)), dma((pieces,)),
            dma((line,)), dma((line,)), dma((line,)), dma((line,)),
            dma((2,)), dma((1,)),
            dma((3,)), dma((2,)),
            dma((nblk,)), dma((nblk,)),
            dma((3,)), dma((3,)),
            dma((line,)), dma((line,)), dma((line,)), dma((line,)),
        ],
        compiler_params=pltpu.CompilerParams(
            collective_id=4, has_side_effects=True, vmem_limit_bytes=60 << 20
        ),
        name="tail",
    )(grad, weights, first, gains, kept, got)


def statistics(values):
    center = values - jnp.mean(values, axis=-1, keepdims=True)
    scale = lax.rsqrt(jnp.mean(jnp.square(center), axis=-1, keepdims=True) + EPSILON)
    return center * scale, scale


def norm_back(grad, xhat, scale, gain):
    eg = grad * gain
    return scale * (
        eg
        - jnp.mean(eg, axis=-1, keepdims=True)
        - xhat * jnp.mean(eg * xhat, axis=-1, keepdims=True)
    )


def split_parts(values):
    high = values.astype(BF16).astype(F32)
    middle = (values - high).astype(BF16).astype(F32)
    return high, middle, values - high - middle


def project_kernel(head_size, tok, first, w_qk, w_v, gain, normed, query, packed, weight):
    pair = 2 * head_size
    cols = 3 * head_size
    width = tok.shape[1]

    @pl.when(pl.program_id(0) == 0)
    def _():
        key, fresh = w_qk[:, cols:], jnp.concatenate([w_v[0], w_v[1]], axis=1)
        weight[:, :pair] = key[:, :pair]
        weight[:, pair : 2 * pair] = fresh[:, :pair]
        weight[:, 2 * pair : 3 * pair] = jnp.concatenate([key[:, pair:], fresh[:, pair:]], axis=1)
        weight[:, 3 * pair :] = jnp.concatenate(
            [w_qk[:, :cols], jnp.zeros((width, WIDTH - cols), BF16)], axis=1
        )

    head = lax.axis_index("head")
    xhat, _ = statistics(tok[...].astype(F32))
    rows = (xhat * gain[...]).astype(BF16)
    normed[...] = rows
    out = dotf(rows, weight[...])
    query[...] = (out[:, 3 * pair :].astype(BF16).astype(F32) * head_size**-0.5).astype(BF16)
    done = out[:, : 3 * pair].astype(BF16)
    kept = jnp.where(lax.rem(head, 2) == 0, first[:, :cols], first[:, cols:])
    given = jnp.concatenate([done[:, :pair], kept[:, :pair], done[:, 2 * pair : 2 * pair + head_size],
                             kept[:, pair:]], axis=1)
    packed[...] = jnp.where(head < 2, done, given)


def project(tok, first, w_qk, w_v, gain, rows=512):
    total, width = tok.shape
    cols = w_qk.shape[1] // 2
    fixed = lambda array: pl.BlockSpec(array.shape, lambda i: (0,) * array.ndim)
    row = lambda n: pl.BlockSpec((rows, n), lambda i: (i, 0))
    return pl.pallas_call(
        functools.partial(project_kernel, HEAD_DIM),
        grid=(total // rows,),
        in_specs=[row(width), row(first.shape[1])] + [fixed(a) for a in (w_qk, w_v, gain)],
        out_specs=[row(width), row(WIDTH), row(2 * cols)],
        out_shape=[
            jax.ShapeDtypeStruct((total, width), BF16),
            jax.ShapeDtypeStruct((total, WIDTH), BF16),
            jax.ShapeDtypeStruct((total, 2 * cols), BF16),
        ],
        scratch_shapes=[pltpu.VMEM((width, 2 * cols + WIDTH), BF16)],
        compiler_params=pltpu.CompilerParams(vmem_limit_bytes=48 << 20),
        cost_estimate=pl.CostEstimate(
            flops=2 * total * width * 640, bytes_accessed=16 << 20, transcendentals=0
        ),
        name="project",
    )(tok, first, w_qk, w_v, gain)


def gelu_both(pre):
    square = pre * pre
    inner = jnp.tanh(GELU_SCALE * (pre + 0.044715 * square * pre))
    slope = GELU_SCALE * (1.0 + 3.0 * 0.044715 * square)
    outer = 0.5 * (1.0 + inner)
    return pre * outer, outer + 0.5 * pre * (1.0 - inner * inner) * slope


def middle_kernel(
    nblk, up_cols, pieces, tok, mixed_parts, cot, gain, rest_own, gathered, query,
    out, grad_resid, grad_wide, gain_part, keep, give, query_later,
    up, down, w_out, up_grad, down_grad, out_grad, mixed, wide_parts, up_got, down_got, out_got,
    sems, out_sems, send_m, recv_m, send_g, recv_g, send_c, recv_c,
    send_z, recv_z, send_y, recv_y,
):
    head, blk = lax.axis_index("head"), lax.axis_index("blk")
    x, core_index = lax.div(head, 2), lax.rem(head, 2)
    core = xor(head, 1)
    others = [xor(head, 2), 3 - head, core]
    odd = lax.rem(blk, 2)
    pair = blk + 1 - 2 * odd
    above, below = lax.rem(blk + 2, nblk), lax.rem(blk + nblk - 2, nblk)
    greet(partners_of(head, blk, nblk, blks=False) + [(head, b) for b in (pair, above, below)])
    heads_of = 4
    part = gathered.shape[2]
    cols = mixed.shape[2]
    heads = cols // HEAD_DIM

    def mixed_copy(i, to, slot):
        return remote(
            mixed_parts.at[to], mixed.at[slot], send_m.at[i], recv_m.at[i], to, blk
        )

    for i, to in enumerate(others):
        mixed_copy(i, to, head).start()
    piece_rows = query.shape[0] // pieces

    def slab(ref, p):
        return ref.at[pl.ds(p * piece_rows, piece_rows)]

    def far_copy(p, to):
        dst = slab(query_later.at[1], p)
        return remote(slab(query, p), dst, send_z.at[p], recv_z.at[p], head, to)

    def near_copy(p, src):
        return remote(src, slab(query_later.at[0], p), send_y.at[p], recv_y.at[p], head, pair)

    for p in range(pieces):

        @pl.when(blk >= 2)
        def _():
            far_copy(p, below).start()

        @pl.when(odd == 1)
        def _():
            near_copy(p, slab(query, p)).start()

    def relay(p):
        @pl.when(blk + 2 < nblk)
        def _():
            far_copy(p, above).wait_recv()

        @pl.when((blk + 2 < nblk) & (odd == 0))
        def _():
            near_copy(p, slab(query_later.at[1], p)).start()

    chunks = [2 * n + 1 - core_index for n in range(2)] + [2 * n + core_index for n in range(2)]

    def load(i, which, own=False):
        target, lo, size = ((w_out, 2 * up_cols, cols), (up, 0, up_cols), (down, up_cols, up_cols))[
            which
        ]
        return [
            pltpu.make_async_copy(
                (rest_own.at[b] if own else gathered.at[chunks[i], b]).at[:, pl.ds(lo, size)],
                target.at[i, pl.ds(b * part, part)],
                sems.at[which, i, b],
            )
            for b in range(nblk)
        ]

    order = [(i, 0) for i in range(heads_of)] + [(i, w) for i in range(heads_of) for w in (1, 2)]
    for i, which in order:
        if i < 2:
            for copy in load(i, which):
                copy.start()
        else:

            @pl.when(x == i - 2)
            def _():
                for copy in load(i, which, True):
                    copy.start()

            @pl.when(x != i - 2)
            def _():
                for copy in load(i, which):
                    copy.start()

    mixed[head] = mixed_parts[head]
    for i in range(heads_of):
        for copy in load(i, 0):
            copy.wait()
    for i, to in enumerate(others):
        mixed_copy(i, to, to).wait_recv()
    branch = None
    for i in range(heads_of):
        term = dotf(mixed[chunks[i]], w_out[i], NT)
        branch = term if branch is None else branch + term
    resid = tok[...].astype(F32) + branch
    xhat, scale = statistics(resid)
    normed = (xhat * gain[...]).astype(BF16)
    cotangent = cot[...]
    total, grad_normed = resid, None

    def to_core(n, k):
        mine, theirs = ((up_grad, up_got), (down_grad, down_got), (out_grad, out_got))[k]
        return remote(mine.at[n], theirs.at[n], send_c.at[k, n], recv_c.at[k, n], core, blk)

    for i in range(heads_of):
        for copy in load(i, 1) + load(i, 2):
            copy.wait()
        pre = dotf(normed, up[i])
        hidden, slope = gelu_both(pre)
        hidden = hidden.astype(BF16)
        grad_pre = (slope * dotf(cotangent, down[i])).astype(BF16)
        total = total + dotf(hidden, down[i], NT)
        term = dotf(grad_pre, up[i], NT)
        grad_normed = term if grad_normed is None else grad_normed + term
        up_grad[i] = dotf(normed, grad_pre, TN).astype(BF16)
        down_grad[i] = dotf(cotangent, hidden, TN).astype(BF16)
        if i < 2:
            to_core(i, 0).start()
            to_core(i, 1).start()
        for p in range(i * pieces // heads_of, (i + 1) * pieces // heads_of):
            relay(p)
    out[...] = total.astype(BF16)
    gain_part[...] = jnp.sum(grad_normed * xhat, axis=0, keepdims=True)
    grad = cotangent.astype(F32) + norm_back(grad_normed, xhat, scale, gain[...])
    grad_resid[...] = grad
    branch_grad = grad.astype(BF16)
    lane = lax.broadcasted_iota(jnp.int32, (tok.shape[0], WIDTH), 1)
    for i in range(heads_of):
        h = chunks[i]
        rows = dotf(branch_grad, w_out[i]).astype(BF16).astype(F32)
        product = rows * mixed[h].astype(F32)
        wide = jnp.concatenate([rows, jnp.zeros((rows.shape[0], WIDTH - cols), F32)], axis=1)
        for k in range(heads):
            delta = jnp.sum(
                product[:, k * HEAD_DIM : (k + 1) * HEAD_DIM], axis=1, keepdims=True
            )
            for c, piece in enumerate(split_parts(-delta)):
                wide = jnp.where(lane == cols + SPLITS * k + c, piece, wide)
        wide_parts[h] = wide.astype(BF16)

    def wide_copy(i, to, slot):
        return remote(
            wide_parts.at[to], grad_wide.at[slot], send_g.at[i], recv_g.at[i], to, blk
        )

    for i, to in enumerate(others):
        wide_copy(i, to, head).start()
    grad_wide[head] = wide_parts[head]
    for i in range(heads_of):
        out_grad[i] = dotf(branch_grad, mixed[chunks[i]], TN).astype(BF16)
        if i < 2:
            to_core(i, 2).start()

    def store(n, k, target):
        mine = (up_grad, down_grad, out_grad)[k]
        lo, size = ((0, up_cols), (up_cols, up_cols), (2 * up_cols, cols))[k]
        return [
            pltpu.make_async_copy(
                mine.at[2 + n, pl.ds(b * part, part)],
                target.at[b].at[:, pl.ds(lo, size)],
                out_sems.at[k, n, b],
            )
            for b in range(nblk)
        ]

    for k in range(3):
        mine, theirs = ((up_grad, up_got), (down_grad, down_got), (out_grad, out_got))[k]
        for n in range(2):
            to_core(n, k).wait_recv()
            mine[2 + n] = (mine[2 + n].astype(F32) + theirs[n].astype(F32)).astype(BF16)

            @pl.when(x == n)
            def _():
                for copy in store(n, k, keep):
                    copy.start()

            @pl.when(x != n)
            def _():
                for copy in store(n, k, give):
                    copy.start()

    for k in range(3):
        for n in range(2):
            for copy in store(n, k, keep):
                copy.wait()
            to_core(n, k).wait_send()
    for i, to in enumerate(others):
        wide_copy(i, to, to).wait_recv()
    for i, to in enumerate(others):
        mixed_copy(i, to, head).wait_send()
        wide_copy(i, to, head).wait_send()
    for p in range(pieces):

        @pl.when((blk + 2 < nblk) | (odd == 0))
        def _():
            near_copy(p, slab(query, p)).wait_recv()

        @pl.when(blk >= 2)
        def _():
            far_copy(p, below).wait_send()

        @pl.when((blk + 2 < nblk) | (odd == 1))
        def _():
            near_copy(p, slab(query, p)).wait_send()


def middle(nblk, tok, mixed_parts, cot, gain, rest_own, gathered, query, up_cols, pieces=8):
    heads_of, rows, cols = mixed_parts.shape
    width = tok.shape[1]
    flops = 2 * rows * width * (6 * up_cols * heads_of + 3 * width)
    dma = pltpu.SemaphoreType.DMA
    vmem = lambda *shape: pltpu.VMEM(shape, BF16)
    return pl.pallas_call(
        functools.partial(middle_kernel, nblk, up_cols, pieces),
        out_shape=[
            jax.ShapeDtypeStruct((rows, width), BF16),
            jax.ShapeDtypeStruct((rows, width), F32),
            jax.ShapeDtypeStruct((heads_of, rows, WIDTH), BF16),
            jax.ShapeDtypeStruct((1, width), F32),
            jax.ShapeDtypeStruct(gathered.shape[1:], BF16),
            jax.ShapeDtypeStruct(gathered.shape[1:], BF16),
            jax.ShapeDtypeStruct((2,) + query.shape, BF16),
        ],
        in_specs=[WHOLE] * 4 + [ANY] * 3,
        out_specs=[WHOLE] * 4 + [ANY] * 3,
        scratch_shapes=[
            vmem(heads_of, width, up_cols), vmem(heads_of, width, up_cols),
            vmem(heads_of, width, cols),
            vmem(heads_of, width, up_cols), vmem(heads_of, width, up_cols),
            vmem(heads_of, width, cols),
            vmem(heads_of, rows, cols), vmem(heads_of, rows, WIDTH),
            vmem(2, width, up_cols), vmem(2, width, up_cols), vmem(2, width, cols),
            dma((3, heads_of, nblk)), dma((3, 2, nblk)),
            dma((3,)), dma((3,)), dma((3,)), dma((3,)), dma((3, 2)), dma((3, 2)),
            dma((pieces,)), dma((pieces,)), dma((pieces,)), dma((pieces,)),
        ],
        compiler_params=pltpu.CompilerParams(
            collective_id=2, has_side_effects=True, vmem_limit_bytes=62 << 20
        ),
        cost_estimate=pl.CostEstimate(
            flops=flops, bytes_accessed=24 << 20, transcendentals=rows * up_cols * heads_of
        ),
        name="middle",
    )(tok, mixed_parts, cot, gain, rest_own, gathered, query)


def pair_sum_kernel(ours, theirs, keep, give):
    odd = lax.rem(lax.axis_index("blk"), 2)
    sums = [(ours[n].astype(F32) + theirs[n].astype(F32)).astype(BF16) for n in range(2)]
    keep[0] = jnp.where(odd == 0, sums[0], sums[1])
    give[0] = jnp.where(odd == 0, sums[1], sums[0])


def pair_sum(ours, theirs):
    nblk, part, width = ours.shape
    both = pl.BlockSpec((2, part, width), lambda i: (i, 0, 0))
    one = pl.BlockSpec((1, part, width), lambda i: (i, 0, 0))
    return pl.pallas_call(
        pair_sum_kernel,
        grid=(nblk // 2,),
        in_specs=[both, both],
        out_specs=[one, one],
        out_shape=[jax.ShapeDtypeStruct((nblk // 2, part, width), BF16)] * 2,
        cost_estimate=pl.CostEstimate(
            flops=nblk * part * width, bytes_accessed=6 * nblk * part * width, transcendentals=0
        ),
        name="pair_sum",
    )(ours, theirs)


def unproject_kernel(
    nblk, d_q, d_k, d_v, normed, gain, w_qk, w_v,
    grad, out_all, gain_part, acc_q, acc_k, acc_v, acc_gain, fresh,
):
    step, last = pl.program_id(0), pl.num_programs(0) - 1
    part = normed.shape[1] // nblk
    cols = d_q.shape[1]

    @pl.when(step == 0)
    def _():
        mine = lax.axis_index("head") < 2
        weight = jnp.concatenate([w_v[0], w_v[1]], axis=1)
        fresh[...] = jnp.where(mine, weight, jnp.zeros_like(weight))
        acc_q[...] = jnp.zeros_like(acc_q)
        acc_k[...] = jnp.zeros_like(acc_k)
        acc_v[...] = jnp.zeros_like(acc_v)
        acc_gain[...] = jnp.zeros_like(acc_gain)

    rows = normed[...]
    mine = lax.axis_index("head") < 2
    d_fresh = jnp.where(mine, d_v[...], jnp.zeros_like(d_v[...]))
    both = jnp.concatenate([d_q[...], d_k[...]], axis=1)
    whole = dotf(both, w_qk[...], NT)
    whole = whole + dotf(d_fresh, fresh[...], NT)
    grad[...] = whole.astype(BF16)
    acc_gain[...] += jnp.sum(whole * rows.astype(F32), axis=0, keepdims=True)
    acc_q[...] += dotf(rows, d_q[...], TN)
    acc_k[...] += dotf(rows, d_k[...], TN)
    acc_v[...] += dotf(rows, d_v[...], TN)

    @pl.when(step == last)
    def _():
        gain_part[...] = acc_gain[...] / gain[...]
        empty = jnp.zeros((normed.shape[1], out_all.shape[2] - 3 * cols), F32)
        whole = jnp.concatenate([acc_q[...], acc_k[...], acc_v[...], empty], axis=1).astype(BF16)
        for b in range(nblk):
            out_all[b] = whole[b * part : (b + 1) * part]


def unproject(nblk, d_q, d_k, d_v, normed, gain, w_qk, w_v, rows=512):
    total, width = normed.shape
    cols = d_q.shape[1]
    part = width // nblk
    fixed = lambda array: pl.BlockSpec(array.shape, lambda i: (0,) * array.ndim)
    row = lambda n: pl.BlockSpec((rows, n), lambda i: (i, 0))
    outs = [
        jax.ShapeDtypeStruct((total, width), BF16),
        jax.ShapeDtypeStruct((nblk, part, -(-3 * cols // 128) * 128), BF16),
        jax.ShapeDtypeStruct((1, width), F32),
    ]
    return pl.pallas_call(
        functools.partial(unproject_kernel, nblk),
        grid=(total // rows,),
        in_specs=[row(cols)] * 3 + [row(width)] + [fixed(a) for a in (gain, w_qk, w_v)],
        out_specs=[row(width)] + [fixed(a) for a in outs[1:]],
        out_shape=outs,
        scratch_shapes=[
            pltpu.VMEM((width, cols), F32),
            pltpu.VMEM((width, cols), F32),
            pltpu.VMEM((width, cols), F32),
            pltpu.VMEM((1, width), F32),
            pltpu.VMEM((width, cols), BF16),
        ],
        compiler_params=pltpu.CompilerParams(vmem_limit_bytes=48 << 20),
        cost_estimate=pl.CostEstimate(
            flops=12 * total * width * cols, bytes_accessed=16 << 20, transcendentals=0
        ),
        name="unproject",
    )(d_q, d_k, d_v, normed, gain, w_qk, w_v)


def head_mask(rows, h, heads, width, dtype=BF16):
    lane=lax.broadcasted_iota(jnp.int32,(rows,width),1)
    real=heads*HEAD_DIM
    m=((lane>=h*HEAD_DIM)&(lane<(h+1)*HEAD_DIM))|((lane>=real+3*h)&(lane<real+3*h+3))
    return m

def doc_start(meta, ndocs, t):
    def step(j,c):
        cum,best=c
        best=jnp.where(cum<=t,cum,best)
        return cum+meta[1+j],best
    return lax.fori_loop(0,ndocs,step,(jnp.int32(0),jnp.int32(0)))[1]

def doc_end(meta, ndocs, t):
    def step(j,c):
        cum,best,found=c
        cum=cum+meta[1+j]
        take=(cum>t)&(found==0)
        return cum,jnp.where(take,cum,best),jnp.where(take,1,found)
    return lax.fori_loop(0,ndocs,step,(jnp.int32(0),jnp.int32(0),jnp.int32(0)))[1]

def starts_vec(meta, ndocs, t):
    def step(j,c):
        cum,best=c
        return cum+meta[1+j],jnp.where(cum<=t,cum,best)
    return lax.fori_loop(0,ndocs,step,(jnp.int32(0),jnp.zeros(t.shape,jnp.int32)))[1]

def ends_vec(meta, ndocs, t):
    def step(j,c):
        cum,best=c
        ln=meta[1+j]
        return cum+ln,jnp.where(cum<=t,cum+ln,best)
    return lax.fori_loop(0,ndocs,step,(jnp.int32(0),jnp.zeros(t.shape,jnp.int32)))[1]

def widened(columns, heads):
    rows, width = columns.shape
    ones = jnp.ones((rows, SPLITS * heads), BF16)
    empty = jnp.zeros((rows, WIDTH - width - SPLITS * heads), BF16)
    return jnp.concatenate([columns, ones, empty], axis=1)


def unpack_rows(packed, heads):
    pair = 2 * HEAD_DIM
    key = jnp.concatenate([packed[:, :pair], packed[:, 2 * pair : 2 * pair + HEAD_DIM]], axis=1)
    value = jnp.concatenate([packed[:, pair : 2 * pair], packed[:, 2 * pair + HEAD_DIM :]], axis=1)
    return widened(key, heads), widened(value, heads)


def build_window(heads, earlier, own, keys, values, step=512):
    block = own.shape[0]
    for j in range(earlier.shape[0] + 1):
        source = own if j == earlier.shape[0] else earlier.at[j]

        @pl.loop(0, block // step)
        def _(i):
            key, value = unpack_rows(source[pl.ds(i * step, step), :], heads)
            at = pl.ds(j * block + i * step, step)
            keys[at, :] = key
            values[at, :] = value


def three(lo,a,b,hi,body):
    lax.fori_loop(lo,a,lambda j,_: body(j,True),None)
    lax.fori_loop(a,b,lambda j,_: body(j,False),None)
    lax.fori_loop(b,hi,lambda j,_: body(j,True),None)

def fwd_kernel(heads, ndocs, tq, tk, meta, q_ref, earlier, own, mix_ref, wide_ref,
               k_ref, v_ref, qh, m_ref, acc_ref):
    i = pl.program_id(0)
    width = q_ref.shape[1]
    real = heads * HEAD_DIM
    base = meta[0]
    wbase = base - earlier.shape[0] * earlier.shape[1]

    @pl.when(i == 0)
    def _():
        build_window(heads, earlier, own, k_ref, v_ref)

    t0 = base + i * tq
    lo = (doc_start(meta, ndocs, t0) - wbase) // tk
    f0 = (doc_start(meta, ndocs, t0 + tq - 1) - wbase + tk - 1) // tk
    f1 = (t0 - wbase) // tk
    hi = (t0 + tq - 1 - wbase) // tk + 1
    f0 = jnp.minimum(f0, f1)
    q = q_ref[...]
    trow = t0 + lax.broadcasted_iota(jnp.int32, (tq, 128), 0)
    srow = starts_vec(meta, ndocs, trow)
    lane = lax.broadcasted_iota(jnp.int32, (tq, width), 1)

    def visible(off):
        u = wbase + off + lax.broadcasted_iota(jnp.int32, (tq, tk), 1)
        return (u >= srow[:, :1]) & (u <= trow[:, :1])

    def with_parts(values):
        wide = q.astype(F32)
        for h in range(heads):
            for c, piece in enumerate(split_parts(values[h])):
                wide = jnp.where(lane == real + SPLITS * h + c, piece, wide)
        return wide.astype(BF16)

    def finish(shifts):
        acc = acc_ref[...]
        out = jnp.zeros((tq, width), F32)
        negated = []
        for h in range(heads):
            total = acc[:, real + SPLITS * h : real + SPLITS * h + 1]
            out = jnp.where(head_mask(tq, h, heads, width), acc / total, out)
            negated.append(-(shifts[h] + jnp.log(total)))
        mix_ref[0] = out[:, :real].astype(BF16)
        wide_ref[...] = with_parts(negated)

    itself = q.astype(F32) * k_ref[pl.ds(pl.multiple_of(t0 - wbase, tq), tq), :].astype(F32)
    shifts = [
        jnp.sum(jnp.where(head_mask(tq, h, heads, width), itself, 0.0), axis=1, keepdims=True)
        for h in range(heads)
    ]
    shifted = with_parts([-x for x in shifts])
    for h in range(heads):
        qh[h] = jnp.where(head_mask(tq, h, heads, width), shifted, jnp.zeros_like(q))
    acc_ref[...] = jnp.zeros_like(acc_ref)

    def quick(j, masked):
        off = pl.multiple_of(j * tk, tk)
        k = k_ref[pl.ds(off, tk), :]
        v = v_ref[pl.ds(off, tk), :]
        if masked:
            vis = visible(off)
        pv = None
        for h in range(heads):
            p = jnp.exp(dotf(qh[h], k, NT))
            if masked:
                p = jnp.where(vis, p, 0.0)
            vh = jnp.where(head_mask(tk, h, heads, width), v, jnp.zeros_like(v))
            d = dotf(p.astype(BF16), vh)
            pv = d if pv is None else pv + d
        acc_ref[...] += pv

    three(lo, f0, f1, hi, quick)
    finish(shifts)
    sums = jnp.where(lane >= real, acc_ref[...], 0.0)
    fits = jnp.max(jnp.where(sums < 1e30, 0.0, 1.0)) == 0.0

    @pl.when(jnp.logical_not(fits))
    def _():
        for h in range(heads):
            qh[h] = jnp.where(head_mask(tq, h, heads, width), q, jnp.zeros_like(q))
            m_ref[h] = jnp.full((tq, 128), EXCLUDED, F32)
        acc_ref[...] = jnp.zeros_like(acc_ref)

        def body(j, carry):
            off = pl.multiple_of(j * tk, tk)
            k = k_ref[pl.ds(off, tk), :]
            v = v_ref[pl.ds(off, tk), :]
            vis = visible(off)
            pv = None
            scale = jnp.ones((tq, width), F32)
            for h in range(heads):
                s = jnp.where(vis, dotf(qh[h], k, NT), EXCLUDED)
                old = m_ref[h][:, :1]
                new = jnp.maximum(old, jnp.max(s, axis=1, keepdims=True))
                m_ref[h] = jnp.broadcast_to(new, (tq, 128))
                scale = jnp.where(head_mask(tq, h, heads, width), jnp.exp(old - new), scale)
                vh = jnp.where(head_mask(tk, h, heads, width), v, jnp.zeros_like(v))
                d = dotf(jnp.exp(s - new).astype(BF16), vh)
                pv = d if pv is None else pv + d
            acc_ref[...] = acc_ref[...] * scale + pv
            return carry

        lax.fori_loop(lo, hi, body, 0)
        finish([m_ref[h][:, :1] for h in range(heads)])


def whole_of(array):
    return pl.BlockSpec(
        array.shape, lambda i: (0,) * array.ndim, pipeline_mode=pl.Buffered(1)
    )


SCALARS = pl.BlockSpec(memory_space=pltpu.SMEM)


def attention_fwd(meta, q, earlier, own, heads, tq, tk):
    block, width = q.shape
    window = block * (1 + earlier.shape[0])
    ndocs = meta.shape[0] - 1
    return pl.pallas_call(
        functools.partial(fwd_kernel, heads, ndocs, tq, tk),
        grid=(block // tq,),
        in_specs=[
            SCALARS,
            pl.BlockSpec((tq, width), lambda i: (i, 0)),
            whole_of(earlier),
            whole_of(own),
        ],
        out_specs=[
            pl.BlockSpec((1, tq, heads * HEAD_DIM), lambda i: (i, 0, 0)),
            pl.BlockSpec((tq, width), lambda i: (i, 0)),
        ],
        out_shape=[
            jax.ShapeDtypeStruct((block // tq, tq, heads * HEAD_DIM), BF16),
            jax.ShapeDtypeStruct((block, width), BF16),
        ],
        scratch_shapes=[
            pltpu.VMEM((window, width), BF16),
            pltpu.VMEM((window, width), BF16),
            pltpu.VMEM((heads, tq, width), BF16),
            pltpu.VMEM((heads, tq, 128), F32),
            pltpu.VMEM((tq, width), F32),
        ],
        compiler_params=pltpu.CompilerParams(vmem_limit_bytes=56 << 20),
        cost_estimate=pl.CostEstimate(
            flops=30_000_000_000, bytes_accessed=12 << 20, transcendentals=20_000_000
        ),
        name="attn_fwd",
    )(meta, q, earlier, own)


def dq_kernel(heads, ndocs, tq, tk, meta, q_ref, do_ref, earlier, own, dq_ref,
              k_ref, v_ref, qh, doh, acc_ref):
    i = pl.program_id(0)
    width = q_ref.shape[1]
    real = heads * HEAD_DIM
    base = meta[0]
    wbase = base - earlier.shape[0] * earlier.shape[1]

    @pl.when(i == 0)
    def _():
        build_window(heads, earlier, own, k_ref, v_ref)

    t0 = base + i * tq
    lo = (doc_start(meta, ndocs, t0) - wbase) // tk
    f0 = (doc_start(meta, ndocs, t0 + tq - 1) - wbase + tk - 1) // tk
    f1 = (t0 - wbase) // tk
    hi = (t0 + tq - 1 - wbase) // tk + 1
    f0 = jnp.minimum(f0, f1)
    q = q_ref[...]
    do = do_ref[...]
    for h in range(heads):
        hm = head_mask(tq, h, heads, width)
        qh[h] = jnp.where(hm, q, jnp.zeros_like(q))
        doh[h] = jnp.where(hm, do, jnp.zeros_like(do))
    acc_ref[...] = jnp.zeros_like(acc_ref)
    trow = t0 + lax.broadcasted_iota(jnp.int32, (tq, 128), 0)
    srow = starts_vec(meta, ndocs, trow)

    def body(j, masked):
        off = pl.multiple_of(j * tk, tk)
        k = k_ref[pl.ds(off, tk), :]
        v = v_ref[pl.ds(off, tk), :]
        if masked:
            u = wbase + off + lax.broadcasted_iota(jnp.int32, (tq, tk), 1)
            vis = (u >= srow[:, :1]) & (u <= trow[:, :1])
        tot = None
        for h in range(heads):
            p = jnp.exp(dotf(qh[h], k, NT))
            if masked:
                p = jnp.where(vis, p, 0.0)
            ds = (p * dotf(doh[h], v, NT)).astype(BF16)
            kh = jnp.where(head_mask(tk, h, heads, width), k, jnp.zeros_like(k))
            d = dotf(ds, kh)
            tot = d if tot is None else tot + d
        acc_ref[...] += tot

    three(lo, f0, f1, hi, body)
    dq_ref[...] = (acc_ref[...] * (HEAD_DIM**-0.5)).astype(BF16)[:, :real]


def attention_dq(meta, q, do, earlier, own, heads, tq, tk):
    block, width = q.shape
    window = block * (1 + earlier.shape[0])
    ndocs = meta.shape[0] - 1
    row = lambda w: pl.BlockSpec((tq, w), lambda i: (i, 0))
    return pl.pallas_call(
        functools.partial(dq_kernel, heads, ndocs, tq, tk),
        grid=(block // tq,),
        in_specs=[SCALARS, row(width), row(width), whole_of(earlier), whole_of(own)],
        out_specs=row(heads * HEAD_DIM),
        out_shape=jax.ShapeDtypeStruct((block, heads * HEAD_DIM), BF16),
        scratch_shapes=[pltpu.VMEM((window, width), BF16)] * 2
        + [pltpu.VMEM((heads, tq, width), BF16)] * 2
        + [pltpu.VMEM((tq, width), F32)],
        compiler_params=pltpu.CompilerParams(vmem_limit_bytes=56 << 20),
        cost_estimate=pl.CostEstimate(
            flops=45_000_000_000, bytes_accessed=12 << 20, transcendentals=20_000_000
        ),
        name="attn_dq",
    )(meta, q, do, earlier, own)


def dkv_kernel(heads, ndocs, tq, tk, meta, own, q_parts, do_parts, dk_ref, dv_ref,
               q_ref, do_ref, kh, vh, dk_acc, dv_acc, sems):
    i = pl.program_id(0)
    width = q_ref.shape[1]
    real = heads * HEAD_DIM
    base = meta[0]

    @pl.when(i == 0)
    def _():
        copies = []
        for k, (parts, target) in enumerate(((q_parts, q_ref), (do_parts, do_ref))):
            row = 0
            for j, part in enumerate(parts):
                at = target.at[pl.ds(row, part.shape[0])]
                copies.append(pltpu.make_async_copy(part, at, sems.at[k, j]))
                row += part.shape[0]
        for copy in copies:
            copy.start()
        for copy in copies:
            copy.wait()

    u0 = base + i * tk
    lo = (u0 - base) // tq
    f0 = (u0 + tk - 1 - base + tq - 1) // tq
    e_first = doc_end(meta, ndocs, u0)
    e_last = doc_end(meta, ndocs, u0 + tk - 1)
    f1 = (e_first - base) // tq
    hi = (e_last - 1 - base) // tq + 1
    f0 = jnp.minimum(f0, hi)
    f1 = jnp.clip(f1, f0, hi)
    k, v = unpack_rows(own[...], heads)
    for h in range(heads):
        hm = head_mask(tk, h, heads, width)
        kh[h] = jnp.where(hm, k, jnp.zeros_like(k))
        vh[h] = jnp.where(hm, v, jnp.zeros_like(v))
    dk_acc[...] = jnp.zeros_like(dk_acc)
    dv_acc[...] = jnp.zeros_like(dv_acc)
    urow = u0 + lax.broadcasted_iota(jnp.int32, (tk, 128), 0)
    erow = ends_vec(meta, ndocs, urow)

    def body(j, masked):
        off = pl.multiple_of(j * tq, tq)
        q = q_ref[pl.ds(off, tq), :]
        do = do_ref[pl.ds(off, tq), :]
        if masked:
            t = base + off + lax.broadcasted_iota(jnp.int32, (tk, tq), 1)
            vis = (t >= urow[:, :1]) & (t < erow[:, :1])
        a = None
        b = None
        for h in range(heads):
            p = jnp.exp(dotf(kh[h], q, NT))
            if masked:
                p = jnp.where(vis, p, 0.0)
            ds = (p * dotf(vh[h], do, NT)).astype(BF16)
            hm = head_mask(tq, h, heads, width)
            d = dotf(p.astype(BF16), jnp.where(hm, do, jnp.zeros_like(do)))
            a = d if a is None else a + d
            d = dotf(ds, jnp.where(hm, q, jnp.zeros_like(q)))
            b = d if b is None else b + d
        dv_acc[...] += a
        dk_acc[...] += b

    three(lo, f0, f1, hi, body)
    dk_ref[...] = dk_acc[...].astype(BF16)[:, :real]
    dv_ref[...] = dv_acc[...].astype(BF16)[:, :real]


def attention_dkv(meta, own, q_parts, do_parts, heads, tq, tk):
    block, width = q_parts[0].shape
    window = sum(part.shape[0] for part in q_parts)
    ndocs = meta.shape[0] - 1
    row = lambda w: pl.BlockSpec((tk, w), lambda i: (i, 0))
    return pl.pallas_call(
        functools.partial(dkv_kernel, heads, ndocs, tq, tk),
        grid=(block // tk,),
        in_specs=[SCALARS, row(own.shape[1]), [ANY] * len(q_parts), [ANY] * len(do_parts)],
        out_specs=[row(heads * HEAD_DIM)] * 2,
        out_shape=[jax.ShapeDtypeStruct((block, heads * HEAD_DIM), BF16)] * 2,
        scratch_shapes=[pltpu.VMEM((window, width), BF16)] * 2
        + [pltpu.VMEM((heads, tk, width), BF16)] * 2
        + [pltpu.VMEM((tk, width), F32)] * 2
        + [pltpu.SemaphoreType.DMA((2, len(do_parts)))],
        compiler_params=pltpu.CompilerParams(vmem_limit_bytes=56 << 20),
        cost_estimate=pl.CostEstimate(
            flops=60_000_000_000, bytes_accessed=12 << 20, transcendentals=20_000_000
        ),
        name="attn_dkv",
    )(meta, own, q_parts, do_parts)


def on_device(
    tokens, first_values, cotangent, w_query, w_key, w_value, w_out, w_up, w_down,
    gain_attn, gain_mlp, doc_lengths,
):
    width = tokens.shape[1]
    heads_of = lax.axis_size("head")
    nblk = lax.axis_size("blk")
    blk = lax.axis_index("blk")
    rows = tokens.shape[0]
    block = rows * heads_of
    heads = HEADS // heads_of
    cols = heads * HEAD_DIM
    part = width // nblk
    meta = jnp.concatenate([jnp.reshape(blk * block, (1,)).astype(jnp.int32), doc_lengths])

    up_cols = w_up.shape[1]
    rest = jnp.concatenate([w_up, w_down.T, w_out.T], axis=1)
    gains = jnp.stack([gain_attn, gain_mlp])[:, None, :]
    tok_all, first_all, qk_all, rest_own, _, v_all, gain_all = front(
        nblk, tokens, first_values, jnp.concatenate([w_query, w_key], axis=1), rest, w_value, gains
    )
    attn_gain = gain_all[:, 0].reshape(1, width)
    mlp_gain = gain_all[:, 1].reshape(1, width)
    w_qk = qk_all.reshape(width, 2 * cols)
    w_v = v_all.reshape(2, width, w_value.shape[1])
    normed, query, own = project(
        tok_all.reshape(block, width), first_all.reshape(block, width // 2), w_qk, w_v, attn_gain
    )
    earlier, gathered = halo(nblk, own, rest_own)
    mixed_parts, query_wide = attention_fwd(meta, query, earlier, own, heads, rows, 2 * rows)
    layer_output, grad_resid, grad_parts, gain_mlp_part, keep, give, query_later = middle(
        nblk, tokens, mixed_parts, cotangent, mlp_gain, rest_own, gathered, query_wide, up_cols
    )
    grad_wide = grad_parts.reshape(block, WIDTH)
    taken = lax.ppermute(give, "head", [(h, (h + 2) % heads_of) for h in range(heads_of)])

    grads_later = [grad_wide] + [
        lax.ppermute(grad_wide, "blk", [(i, i - d) for i in range(d, nblk)]) for d in (1, 2)
    ]
    queries_later = [query_wide, query_later.reshape(2 * block, WIDTH)]
    grad_query = attention_dq(meta, query_wide, grad_wide, earlier, own, heads, rows, rows)
    taken, keep, grad_query = lax.optimization_barrier((taken, keep, grad_query))
    keep, give = pair_sum(keep, taken)
    taken = lax.ppermute(give, "blk", [(i, i + 1 - 2 * (i % 2)) for i in range(nblk)])
    keep, own = lax.optimization_barrier((keep, own))
    grad_key, grad_value = attention_dkv(
        meta, own, queries_later, grads_later, heads, rows, rows
    )
    grad_normed, part_weights, gain_attn_part = unproject(
        nblk, grad_query, grad_key, grad_value, normed, attn_gain, w_qk, w_v
    )
    gain_parts = jnp.concatenate([gain_attn_part, gain_mlp_part]).reshape(2, nblk, 1, part)
    grad_norm_sum, final_qk, final_value, first_parts, gain_sums, reduced = tail(
        nblk,
        grad_normed.reshape(heads_of, rows, width),
        part_weights,
        grad_value.reshape(heads_of, rows, cols),
        gain_parts.transpose(1, 0, 2, 3),
        keep,
        taken,
        cols,
    )
    xhat, scale1 = statistics(tokens.astype(F32))
    grad_tokens = grad_resid + norm_back(grad_norm_sum, xhat, scale1, attn_gain)
    grad_first = jnp.concatenate([first_parts[0], first_parts[1]], axis=1).astype(F32)
    return (
        layer_output,
        grad_tokens,
        grad_first,
        final_qk[:, :cols],
        final_qk[:, cols:],
        final_value,
        reduced[:, 2 * up_cols :].T,
        reduced[:, :up_cols],
        reduced[:, up_cols : 2 * up_cols].T,
        gain_sums[0].reshape(part),
        gain_sums[1].reshape(part),
    )


def solution(mesh):
    rows = P(("blk", "head"), None)
    specs = (P("blk", "head"),) * 3 + (P("head", "blk"), P("blk", "head"), P("head", "blk"))
    gains = (P("blk"), P("blk"))
    return jax.shard_map(
        on_device,
        mesh=mesh,
        in_specs=(rows,) * 3 + specs + gains + (P(),),
        out_specs=(rows,) * 3 + specs + gains,
        check_vma=False,
    )
```

time: 627 us -> 463 us (0.74)
  local copies, waits for them, and re-layouts: 96 us -> 21.3 us
  matrix products: 64.6 us -> 0 us
  other arithmetic: 68.8 us -> 8.99 us
  Pallas kernels: 326 us -> 378 us
  between operations: 15.2 us -> 1.07 us
  waiting for transfers between devices: 44.6 us -> 38.3 us
    pallas_call x6 -> x8, Pallas kernels: 220 us -> 285 us  [the longest x1 86.4 us: tail(): pl.pallas_call(functools.partial(tail_kernel, nblk, pieces, cols), out_sh...]
    dot_general x18 -> x0, matrix products: 64.6 us -> none  [dotf(): return lax.dot_general(left, right, dims, preferred_element_type=F32)]
    concatenate x9 -> x3, other arithmetic: 46.9 us -> 3.29 us  [the longest x1 1.74 us: on_device(): rest = jnp.concatenate([w_up, w_down.T, w_out.T], axis=1)]
    reshape x9 -> x2, local copies, waits for them, and re-layouts: 30.3 us -> 0.69 us  [on_device(): jnp.concatenate([gain_attn_part, gain_mlp_part]).reshape(2, nblk, 1, part)]
    slice x12 -> x2, local copies, waits for them, and re-layouts: 18 us -> 2.55 us  [the longest x1 1.84 us: on_device(): final_qk[:, cols:]]
    unnamed x134 -> x52, local copies, waits for them, and re-layouts: 26.2 us -> 14.8 us
    pallas_call x1, Pallas kernels: 51 us -> 41.4 us  [attention_dkv(): pl.pallas_call(functools.partial(dkv_kernel, heads, ndocs, tq, tk), grid=...]
    convert_element_type x5 -> x0, local copies, waits for them, and re-layouts: 9.53 us -> none  [the longest x1 6.63 us: repacked(): whole.astype(BF16).reshape(nblk, part, heads_of, whole.shape[1] // heads_of)]
  transfers between devices with their start and end apart: 6 -> 4, of which waited for: 1 -> 1; matrix products, arithmetic and copies ran while one was open for 25% -> 0% of each run, Pallas kernels for 50% -> 17%
where the time goes in v2:
time: 463 us; the launch traced here: 455 us
  Pallas kernels  378 us (82%)
  waiting for transfers between devices  38.3 us (8%)
  local copies, waits for them, and re-layouts  21.3 us (5%)
  other arithmetic  8.99 us (2%)
  starting transfers between devices  7.03 us (2%)
    pallas_call x1, Pallas kernels, tail(): pl.pallas_call(functools.partial(tail_kernel, nblk, pieces, cols), out_sh...  86.4 us
    pallas_call x1, Pallas kernels, middle(): pl.pallas_call(functools.partial(middle_kernel, nblk, up_cols, pieces), o...  65.8 us
    pallas_call x1, Pallas kernels, halo(): pl.pallas_call(functools.partial(halo_kernel, nblk, pieces), out_shape=[j...  64.7 us
    pallas_call x1, Pallas kernels, front(): pl.pallas_call(functools.partial(front_kernel, nblk, pieces), out_shape=[...  52.3 us
    pallas_call x1, Pallas kernels, attention_dkv(): pl.pallas_call(functools.partial(dkv_kernel, heads, ndocs, tq, tk), grid=...  41.4 us
    ppermute x1, waiting for transfers between devices, on_device(): lax.ppermute(give, 'head', [(h, (h + 2) % heads_of) for h in range(heads_...  38.3 us
    pallas_call x1, Pallas kernels, attention_fwd(): pl.pallas_call(functools.partial(fwd_kernel, heads, ndocs, tq, tk), grid=...  25.8 us
    pallas_call x1, Pallas kernels, attention_dq(): pl.pallas_call(functools.partial(dq_kernel, heads, ndocs, tq, tk), grid=(...  22.2 us
  transfers between devices with their start and end apart: 4, of which 1 were waited for; matrix products, arithmetic and copies ran while one was open for 0% of the time, Pallas kernels for 17%

profile of v2, /device:TPU:0, one launch (start us, length us, event | category | flops | bytes accessed | tf_op | source)
XLA Modules:
  0.0 455.1 jit_solution(14594529190640403025)
XLA Ops:
  0.6 0.9 copy.25
  1.5 1.5 pad_maximum_fusion.1.w_qk
  3.1 1.2 pad_maximum_fusion.3
  4.3 1.7 pad_maximum_fusion.w_rest
  6.1 52.3 %front.1 = (bf16[4,512,768]{2,1,0:T(8,128)(2,1)}, bf16[4,512,384]{2,1,0:T(8,128)(2,1)}, bf16[8,96,384]{2,1,0:T(8,128)(2,1)}, bf16[8,96,1728]{2,1,0:T(8,128)(2,1)...) custom-call(bf16[512,768]{1,0:T(8,128)(2,1)} %tok.3, ...), custom_call_target="tpu_custom_call" | custom-call | tf_op jit(solution)/shard_map/front/pallas_call | solution.py:276
  58.4 0.7 slice_reduce_fusion
  59.1 0.1 reshape_squeeze.12.gain
  59.2 0.7 reshape_squeeze.13.gain
  59.9 1.4 copy-done.5
  61.3 1.1 copy-done.6
  62.3 1.0 copy-done.8
  63.3 6.5 %project.1 = (bf16[2048,768]{1,0:T(8,128)(2,1)}, bf16[2048,256]{1,0:T(8,128)(2,1)S(1)}, bf16[2048,384]{1,0:T(8,128)(2,1)S(1)}) custom-call(bf16[2048,768]{1,0:T(8,128)(2,1)} %bitcast.44, bf16[2048,384]{1,0:T(8,128)(2,1)S(1)} %bitcast.31, bf16[768,384]{1,0:T(8,128)(2,1)S(1)} %bitcast.32, bf16[2,768,96]{2,1,0:T(8,128)(2,1)S(1)} %bitcast.34, ...), custom_call_target="tpu_custom_call" | custom-call | flops 2013265920 | bytes 16777216 | tf_op jit(solution)/shard_map/project/pallas_call | solution.py:724
  69.8 1.1 copy-done
  71.0 1.0 copy-done.10
  71.9 64.7 %halo.1 = (bf16[2,2048,384]{2,1,0:T(8,128)(2,1)}, bf16[4,8,96,1728]{3,2,1,0:T(8,128)(2,1)}) custom-call(bf16[2048,384]{1,0:T(8,128)(2,1)} %copy-done, bf16[8,96,1728]{2,1,0:T(8,128)(2,1)} %get-tuple-element.56.rest.rest_own), custom_call_target="tpu_custom_call" | custom-call | tf_op jit(solution)/shard_map/halo/pallas_call | solution.py:379
  136.6 0.6 pad_add_fusion.meta
  137.2 25.8 %attn_fwd.1 = (bf16[4,512,192]{2,1,0:T(8,128)(2,1)}, bf16[2048,256]{1,0:T(8,128)(2,1)}) custom-call(s32[17]{0:T(128)} %pad_add_fusion.meta, bf16[2048,256]{1,0:T(8,128)(2,1)} %copy-done.10, bf16[2,2048,384]{2,1,0:T(8,128)(2,1)} %get-tuple-element.57.earlier, bf16[2048,384]{1,0:T(8,128)(2,1)} %copy-done), custom_call_target="tpu_custom_call" | custom-call | flops 30000001024 | bytes 12582912 | tf_op jit(solution)/shard_map/attn_fwd/pallas_call | solution.py:1283
  163.1 65.8 %middle.1 = (bf16[512,768]{1,0:T(8,128)(2,1)}, f32[512,768]{1,0:T(8,128)}, bf16[4,512,256]{2,1,0:T(8,128)(2,1)}, f32[1,768]{1,0:T(1,128)}, bf16[8,96,1728]{2,1,0...) custom-call(bf16[512,768]{1,0:T(8,128)(2,1)} %tok.3, ...), custom_call_target="tpu_custom_call" | custom-call | flops 16307453952 | bytes 25165824 | tf_op jit(solution)/shard_map/middle/pallas_call | solution.py:969
  228.9 1.3 collective-permute-start.1
  230.2 1.3 collective-permute-start.2
  231.5 1.5 collective-permute-start
  233.0 22.2 %attn_dq.1.d_q = bf16[2048,192]{1,0:T(8,128)(2,1)} custom-call(s32[17]{0:T(128)} %pad_add_fusion.meta, bf16[2048,256]{1,0:T(8,128)(2,1)} %get-tuple-element.60.query.q_ref.q_parts_0_, bf16[2048,256]{1,0:T(8,128)(2,1)} %bitcast.47, bf16[2,2048,384]{2,1,0:T(8,128)(2,1)} %get-tuple-element.57.earlier, bf16[2048,384]{1,0:T(8,128)(2,1)} %copy-done), custom_call_target="tpu_custom_call" | custom-call | flops 44999999488 | bytes 12582912 | tf_op jit(solution)/shard_map/attn_dq/pallas_call | solution.py:1370
  255.2 0.1 mul.40
  255.3 0.2 convert_reduce_fusion
  255.5 0.4 fusion.8
  255.9 38.3 %collective-permute-done.theirs = bf16[8,96,1728]{2,1,0:T(8,128)(2,1)S(1)} collective-permute-done((bf16[8,96,1728]{2,1,0:T(8,128)(2,1)}, bf16[8,96,1728]{2,1,0:T(8,128)(2,1)S(1)}, u32[]{:S(2)}, u32[]{:S(2)}) %collective-permute-start) | collective-permute-done | bytes 2654240 | tf_op jit(solution)/shard_map/ppermute | solution.py:1511
  294.2 1.5 copy-done.15
  295.7 4.9 %pair_sum.1 = (bf16[4,96,1728]{2,1,0:T(8,128)(2,1)}, bf16[4,96,1728]{2,1,0:T(8,128)(2,1)}) custom-call(bf16[8,96,1728]{2,1,0:T(8,128)(2,1)} %get-tuple-element.67.ours, bf16[8,96,1728]{2,1,0:T(8,128)(2,1)} %copy-done.15), custom_call_target="tpu_custom_call" | custom-call | flops 1327104 | bytes 7962624 | tf_op jit(solution)/shard_map/pair_sum/pallas_call | solution.py:1014
  300.5 3.0 collective-permute-start.3
  303.5 41.4 %attn_dkv.1 = (bf16[2048,192]{1,0:T(8,128)(2,1)}, bf16[2048,192]{1,0:T(8,128)(2,1)}) custom-call(s32[17]{0:T(128)} %pad_add_fusion.meta, bf16[2048,384]{1,0:T(8,128)(2,1)} %copy-done, bf16[2048,256]{1,0:T(8,128)(2,1)} %get-tuple-element.60.query.q_ref.q_parts_0_, bf16[4096,256]{1,0:T(8,128)(2,1)} %bitcast.49, bf16[2048,256]{1,0:T(8,128)(2,1)} %bitcast.48, ...), custom_call_target="tpu_custom_call" | custom-call | flops 60000002048 | bytes 12582912 | tf_op jit(solution)/shard_map/attn_dkv/pallas_call | solution.py:1459
  345.0 1.2 copy-done.1
  346.2 1.2 copy-done.12
  347.4 8.4 %unproject.1 = (bf16[2048,768]{1,0:T(8,128)(2,1)}, bf16[8,96,640]{2,1,0:T(8,128)(2,1)S(1)}, f32[1,768]{1,0:T(1,128)S(1)}) custom-call(bf16[2048,192]{1,0:T(8,128)(2,1)S(1)} %copy-done.11, bf16[2048,192]{1,0:T(8,128)(2,1)S(1)} %copy-done.12, bf16[2048,192]{1,0:T(8,128)(2,1)S(1)} %copy-done.1, bf16[2048,768]{1,0:T(8,128)(2,1)} %get-tuple-element.74.normed, ...), custom_call_target="tpu_custom_call" | custom-call | flops 3623878656 | bytes 16777216 | tf_op jit(solution)/shard_map/unproject/pallas_call | solution.py:1077
  355.8 0.9 copy-done.2
  356.8 0.1 reshape.82
  356.8 0.6 copy.29
  357.4 1.1 copy-done.17
  358.5 86.4 %tail.1 = (f32[512,768]{1,0:T(8,128)}, f32[96,384]{1,0:T(8,128)}, f32[96,96]{1,0:T(8,128)}, bf16[2,512,192]{2,1,0:T(8,128)(2,1)}, f32[2,1,96]{2,1,0:T(1,128)}, /*index=5*/f32[96,1728]{1,0:T(8,128)}) custom-call(bf16[4,512,768]{2,1,0:T(8,128)(2,1)} %bitcast.36, bf16[8,96,640]{2,1,0:T(8,128)(2,1)} %copy-done.2, bf16[4,512,192]{2,1,0:T(8,128)(2,1)} %bitcast.30, ...), custom_call_target="tpu_custom_call" | custom-call | tf_op jit(solution)/shard_map/tail/pallas_call | solution.py:631
  444.9 2.0 slice_bitcast_fusion
  446.9 1.8 fusion.9
  448.7 0.7 copy.27
  449.5 0.5 slice_bitcast_fusion.4
  450.0 1.0 maximum_convert_fusion
  451.1 0.6 multiply_reduce_fusion
  451.7 0.1 copy-done.16
  451.7 1.7 fusion.7
  453.4 0.9 copy.32
  454.3 0.6 copy.33
  (45 shorter events, 0.1 us)
Async XLA Ops:
  59.2 10.6 %copy-start.3 = (f32[1,768]{1,0:T(1,128)}, f32[1,768]{1,0:T(1,128)S(1)}, u32[]{:S(2)}) copy-start(f32[1,768]{1,0:T(1,128)S(1)} %reshape_squeeze.12.gain) | copy-start | bytes 9220
  59.9 1.4 copy-start.5
  61.3 1.1 copy-start.6
  62.3 1.0 copy-start.8
  69.8 1.1 copy-start
  71.0 1.0 copy-start.10
  71.9 64.7 %copy-start.23 = (s32[16]{0:T(128)S(1)}, s32[16]{0:T(128)}, u32[]{:S(2)}) copy-start(s32[16]{0:T(128)} %param.23) | copy-start | bytes 196
  228.9 74.6 %collective-permute-start.1 = (bf16[2048,256]{1,0:T(8,128)(2,1)}, bf16[2048,256]{1,0:T(8,128)(2,1)}, u32[]{:S(2)}, u32[]{:S(2)}) collective-permute-start(bf16[2048,256]{1,0:T(8,128)(2,1)} %bitcast.45), channel_id=1, source_target_pairs={{1,0},{2,1},{3,2},{4,3},{5,4},{6,5},{7,6},{9,8},{10,9},{11,10},{12... | collective-permute-start | bytes 3145736 | tf_op jit(solution)/shard_map/ppermute | solution.py:1514
  230.2 73.3 %collective-permute-start.2 = (bf16[2048,256]{1,0:T(8,128)(2,1)}, bf16[2048,256]{1,0:T(8,128)(2,1)}, u32[]{:S(2)}, u32[]{:S(2)}) collective-permute-start(bf16[2048,256]{1,0:T(8,128)(2,1)} %bitcast.46), channel_id=1, source_target_pairs={{2,0},{3,1},{4,2},{5,3},{6,4},{7,5},{10,8},{11,9},{12,10},{13,11},... | collective-permute-start | bytes 3145736 | tf_op jit(solution)/shard_map/ppermute | solution.py:1514
  231.5 23.8 %copy-start.13 = (bf16[512,768]{1,0:T(8,128)(2,1)S(1)}, bf16[512,768]{1,0:T(8,128)(2,1)}, u32[]{:S(2)}) copy-start(bf16[512,768]{1,0:T(8,128)(2,1)} %tok.3) | copy-start | bytes 2359300
  231.5 62.7 %collective-permute-start = (bf16[8,96,1728]{2,1,0:T(8,128)(2,1)}, bf16[8,96,1728]{2,1,0:T(8,128)(2,1)S(1)}, u32[]{:S(2)}, u32[]{:S(2)}) collective-permute-start(bf16[8,96,1728]{2,1,0:T(8,128)(2,1)} %get-tuple-element.63), channel_id=1, source_target_pairs={{0,16},{8,24},{16,0},{24,8},{1,17},{9,25},{17,1},{25,9},{2,18},{10... | collective-permute-start | bytes 7962632 | tf_op jit(solution)/shard_map/ppermute | solution.py:1511
  294.2 1.5 copy-start.15
  300.5 56.9 %collective-permute-start.3 = (bf16[4,96,1728]{2,1,0:T(8,128)(2,1)}, bf16[4,96,1728]{2,1,0:T(8,128)(2,1)S(1)}, u32[]{:S(2)}, u32[]{:S(2)}) collective-permute-start(bf16[4,96,1728]{2,1,0:T(8,128)(2,1)} %get-tuple-element.80), channel_id=1, source_target_pairs={{0,1},{1,0},{2,3},{3,2},{4,5},{5,4},{6,7},{7,6},{8,9},{9,8},{10,11... | collective-permute-start | bytes 3981320 | tf_op jit(solution)/shard_map/ppermute | solution.py:1520
  303.5 41.4 %copy-start.4 = (f32[1,768]{1,0:T(1,128)S(1)}, f32[1,768]{1,0:T(1,128)}, u32[]{:S(2)}) copy-start(f32[1,768]{1,0:T(1,128)} %copy-done.3) | copy-start | bytes 9220
  303.5 41.4 %copy-start.7 = (bf16[8,96,384]{2,1,0:T(8,128)(2,1)S(1)}, bf16[8,96,384]{2,1,0:T(8,128)(2,1)}, u32[]{:S(2)}) copy-start(bf16[8,96,384]{2,1,0:T(8,128)(2,1)} %get-tuple-element.51) | copy-start | bytes 1769476
  303.5 41.4 %copy-start.9 = (bf16[2,8,96,96]{3,2,1,0:T(8,128)(2,1)S(1)}, bf16[2,8,96,96]{3,2,1,0:T(8,128)(2,1)}, u32[]{:S(2)}) copy-start(bf16[2,8,96,96]{3,2,1,0:T(8,128)(2,1)} %get-tuple-element.52) | copy-start | bytes 884740
  303.5 41.4 %copy-start.11 = (bf16[2048,192]{1,0:T(8,128)(2,1)S(1)}, bf16[2048,192]{1,0:T(8,128)(2,1)}, u32[]{:S(2)}) copy-start(bf16[2048,192]{1,0:T(8,128)(2,1)} %attn_dq.1.d_q) | copy-start | bytes 2359300
  345.0 1.2 copy-start.1
  346.2 1.2 copy-start.12
  347.4 9.3 %copy-start.21 = (f32[1,768]{1,0:T(1,128)S(1)}, f32[1,768]{1,0:T(1,128)}, u32[]{:S(2)}) copy-start(f32[1,768]{1,0:T(1,128)} %get-tuple-element.78) | copy-start | bytes 9220
  355.8 0.9 copy-start.2
  357.4 1.1 copy-start.17
  444.9 4.6 %copy-start.19 = (bf16[2,512,192]{2,1,0:T(8,128)(2,1)S(1)}, bf16[2,512,192]{2,1,0:T(8,128)(2,1)}, u32[]{:S(2)}) copy-start(bf16[2,512,192]{2,1,0:T(8,128)(2,1)} %get-tuple-element.82) | copy-start | bytes 1179652
  444.9 4.6 %copy-start.22 = (f32[2,1,96]{2,1,0:T(1,128)S(1)}, f32[2,1,96]{2,1,0:T(1,128)}, u32[]{:S(2)}) copy-start(f32[2,1,96]{2,1,0:T(1,128)} %get-tuple-element.86) | copy-start | bytes 2308
  446.9 4.2 copy-start.14
  450.0 1.7 copy-start.16
  451.7 1.7 copy-start.18
  453.4 0.9 copy-start.20
